TPU v7x, 32 devices: a whole 2x2x4 slice. The times are simulated.
32 devices in a mesh: dp: 4 (over z), mp: 8 (over y, x, core).
Axes of the slice: x: 2, y: 2, z: 4, core: 2. Of those that a mesh axis runs over, the one named last changes fastest.
Arguments:
- layer_input: bfloat16 [4096, 2048], P(('dp', 'mp')), may hold values from -6 to 6
- lengths: int32 [4, 4], P('dp'), may hold values from 1 to 512, 1024 in all within a row
- norm1_gain: float32 [2048], replicated, may hold values from 0.5 to 1.5
- norm1_bias: float32 [2048], replicated, may hold values from -3 to 3
- norm2_gain: float32 [2048], replicated, may hold values from 0.5 to 1.5
- norm2_bias: float32 [2048], replicated, may hold values from -3 to 3
- qkv_weight: bfloat16 [2048, 6144], P(None, 'mp'), may hold values from -0.125 to 0.125
- qkv_bias: float32 [6144], P('mp'), may hold values from -3 to 3
- out_weight: bfloat16 [2048, 2048], P('mp'), may hold values from -1 to 1
- out_bias: float32 [2048], replicated, may hold values from -3 to 3
- up_weight: bfloat16 [2048, 8192], P(None, 'mp'), may hold values from -0.125 to 0.125
- up_bias: float32 [8192], P('mp'), may hold values from -3 to 3
- down_weight: bfloat16 [8192, 2048], P('mp'), may hold values from -0.0625 to 0.0625
- down_bias: float32 [2048], replicated, may hold values from -3 to 3
- cotangent: bfloat16 [4096, 2048], P(('dp', 'mp')), may hold values from -6 to 6
Outputs:
- layer_output: bfloat16 [4096, 2048], P(('dp', 'mp'))
- input_grad: float32 [4096, 2048], P(('dp', 'mp'))
- norm1_gain_grad: float32 [2048], replicated
- norm1_bias_grad: float32 [2048], replicated
- norm2_gain_grad: float32 [2048], replicated
- norm2_bias_grad: float32 [2048], replicated
- qkv_weight_grad: float32 [2048, 6144], P(None, 'mp')
- qkv_bias_grad: float32 [6144], P('mp')
- out_weight_grad: float32 [2048, 2048], P('mp')
- out_bias_grad: float32 [2048], replicated
- up_weight_grad: float32 [2048, 8192], P(None, 'mp')
- up_bias_grad: float32 [8192], P('mp')
- down_weight_grad: float32 [8192, 2048], P('mp')
- down_bias_grad: float32 [2048], replicated
Inputs may be any that keep to these rules, and one draw needn't show every extreme that they name: In each row of lengths the 4 entries sum to 1024 and the largest is 512.
All inputs are finite; a program needn't handle non-finite values.
Results may differ from a plain program's by a relative error of at most 0.012.
Values may be sent and summed in bfloat16 or wider, within the bound.
No kernel may reach another device: no remote copies, remote signals or barrier semaphores. Data moves between devices by JAX's collectives and lax.ppermute only.
A program may use at most 192 MiB of HBM per device.

v0:
```python
import jax
import jax.numpy as jnp
from jax import lax
from jax.sharding import PartitionSpec as P

HEAD_DIM = 128
ROTARY = 32


norm_eps = 1e-05
masked_score = -1e30
inv_root_two = 0.7071067811865476
inv_root_tau = 0.3989422804014327


def contract_rows(left, right):
    return lax.dot_general(
        left, right, (((0,), (0,)), ((), ())), preferred_element_type=jnp.float32
    )


def contract_cols(left, right):
    return lax.dot_general(
        left, right, (((1,), (1,)), ((), ())), preferred_element_type=jnp.float32
    )


def layer_norm(values_in, norm_gain, norm_bias):
    row_mean = jnp.mean(values_in, axis=-1, keepdims=True)
    centred = values_in - row_mean
    variance = jnp.mean(centred * centred, axis=-1, keepdims=True)
    return centred * lax.rsqrt(variance + norm_eps) * norm_gain + norm_bias


def norm_stats(values_in):
    row_mean = jnp.mean(values_in, axis=-1, keepdims=True)
    centred = values_in - row_mean
    variance = jnp.mean(centred * centred, axis=-1, keepdims=True)
    inv_std = lax.rsqrt(variance + norm_eps)
    return (centred * inv_std, inv_std)


def norm_apply_back(normed, inv_std, scaled):
    return inv_std * (
        scaled
        - jnp.mean(scaled, axis=-1, keepdims=True)
        - normed * jnp.mean(scaled * normed, axis=-1, keepdims=True)
    )


def layout(seq_lengths, group_rows):
    seq_ends = jnp.cumsum(seq_lengths)
    seq_starts = seq_ends - seq_lengths
    places = jnp.arange(group_rows, dtype=jnp.int32)
    segment = jnp.sum((places[:, None] >= seq_ends[None, :]).astype(jnp.int32), axis=1)
    seq_first = jnp.max(
        jnp.where(seq_starts[None, :] <= places[:, None], seq_starts[None, :], 0), axis=1
    )
    return (places, segment, places - seq_first)


def rotary_tables(position):
    half_rot = ROTARY // 2
    frequency = 10000.0 ** (-2.0 * jnp.arange(half_rot, dtype=jnp.float32) / ROTARY)
    angles = position.astype(jnp.float32)[:, None] * frequency[None, :]
    cos_half = jnp.cos(angles)
    sine_half = jnp.sin(angles)
    return (
        jnp.concatenate([cos_half, cos_half], axis=1),
        jnp.concatenate([sine_half, sine_half], axis=1),
    )


def rotate(values_in, cos_table, sine_table):
    half_rot = ROTARY // 2
    rot_part = values_in[..., :ROTARY]
    turned = jnp.concatenate([-rot_part[..., half_rot:], rot_part[..., :half_rot]], axis=-1)
    return jnp.concatenate(
        [rot_part * cos_table + turned * sine_table, values_in[..., ROTARY:]], axis=-1
    )


def rotate_back(grad_in, cos_table, sine_table):
    half_rot = ROTARY // 2
    rot_part = grad_in[..., :ROTARY]
    moved = rot_part * sine_table
    swapped = jnp.concatenate([moved[..., half_rot:], -moved[..., :half_rot]], axis=-1)
    return jnp.concatenate([rot_part * cos_table + swapped, grad_in[..., ROTARY:]], axis=-1)


def allowed_block(places, segment, first_row, last_row):
    same_seq = segment[first_row:last_row, None] == segment[None, :last_row]
    earlier = places[None, :last_row] <= places[first_row:last_row, None]
    return same_seq & earlier


def per_device(
    layer_input,
    lengths,
    norm1_gain,
    norm1_bias,
    norm2_gain,
    norm2_bias,
    qkv_weight,
    qkv_bias,
    out_weight,
    out_bias,
    up_weight,
    up_bias,
    down_weight,
    down_bias,
    cotangent,
):
    input_float = layer_input.astype(jnp.float32)
    first_own = layer_norm(input_float, norm1_gain, norm1_bias).astype(jnp.bfloat16)
    second_own = layer_norm(input_float, norm2_gain, norm2_bias).astype(jnp.bfloat16)
    first_all, second_all = (
        lax.all_gather(first_own, "mp", axis=0, tiled=True),
        lax.all_gather(second_own, "mp", axis=0, tiled=True),
    )
    group_rows = first_all.shape[0]
    heads_local = out_weight.shape[0] // HEAD_DIM
    places, segment, position = layout(lengths[0], group_rows)
    cos_table, sine_table = rotary_tables(position)
    block_rows = max(min(512, group_rows), group_rows // 8)
    block_count = group_rows // block_rows
    score_scale = HEAD_DIM ** (-0.5)
    qkv_raw = jnp.dot(first_all, qkv_weight, preferred_element_type=jnp.float32) + qkv_bias
    qkv_raw = qkv_raw.reshape(group_rows, heads_local, 3, HEAD_DIM)
    queries = jnp.transpose(
        rotate(qkv_raw[:, :, 0], cos_table[:, None, :], sine_table[:, None, :]), (1, 0, 2)
    ).astype(jnp.bfloat16)
    keys_all = jnp.transpose(
        rotate(qkv_raw[:, :, 1], cos_table[:, None, :], sine_table[:, None, :]), (1, 0, 2)
    ).astype(jnp.bfloat16)
    values = jnp.transpose(qkv_raw[:, :, 2], (1, 0, 2)).astype(jnp.bfloat16)

    def block_scores(head_index, first_row, last_row):
        raw_scores = (
            contract_cols(queries[head_index, first_row:last_row], keys_all[head_index, :last_row])
            * score_scale
        )
        return jnp.where(
            allowed_block(places, segment, first_row, last_row), raw_scores, masked_score
        )

    head_outputs = []
    head_logs = []
    for head_index in range(heads_local):
        out_pieces = []
        log_pieces = []
        for block_index in range(block_count):
            first_row = block_index * block_rows
            last_row = first_row + block_rows
            scores = block_scores(head_index, first_row, last_row)
            row_peak = jnp.max(scores, axis=1, keepdims=True)
            row_exp = jnp.exp(scores - row_peak)
            row_total = jnp.sum(row_exp, axis=1, keepdims=True)
            probs_low = (row_exp / row_total).astype(jnp.bfloat16)
            out_pieces.append(
                jnp.dot(
                    probs_low, values[head_index, :last_row], preferred_element_type=jnp.float32
                ).astype(jnp.bfloat16)
            )
            log_pieces.append(row_peak + jnp.log(row_total))
        head_outputs.append(jnp.concatenate(out_pieces, axis=0))
        head_logs.append(jnp.concatenate(log_pieces, axis=0))
    attended = jnp.concatenate(head_outputs, axis=1)
    gate_pre = jnp.dot(second_all, up_weight, preferred_element_type=jnp.float32) + up_bias
    hidden = jax.nn.gelu(gate_pre, approximate=False).astype(jnp.bfloat16)
    branch = lax.psum_scatter(
        jnp.dot(attended, out_weight, preferred_element_type=jnp.float32)
        + jnp.dot(hidden, down_weight, preferred_element_type=jnp.float32),
        "mp",
        scatter_dimension=0,
        tiled=True,
    )
    layer_output = (input_float + branch + out_bias + down_bias).astype(jnp.bfloat16)
    grad_out = lax.all_gather(cotangent, "mp", axis=0, tiled=True)
    out_weight_grad = contract_rows(attended, grad_out)
    down_weight_grad = contract_rows(hidden, grad_out)
    out_bias_grad = jnp.sum(grad_out, axis=0, dtype=jnp.float32)
    grad_attended = contract_cols(grad_out, out_weight).astype(jnp.bfloat16)
    grad_hidden = contract_cols(grad_out, down_weight)
    slope = (
        0.5 * (1.0 + lax.erf(gate_pre * inv_root_two))
        + gate_pre * jnp.exp(-0.5 * gate_pre * gate_pre) * inv_root_tau
    )
    grad_gate = (grad_hidden * slope).astype(jnp.bfloat16)
    up_weight_grad = contract_rows(second_all, grad_gate)
    up_bias_grad = jnp.sum(grad_gate, axis=0, dtype=jnp.float32)
    second_grad = contract_cols(grad_gate, up_weight)
    head_grads = []
    for head_index in range(heads_local):
        grad_heads = grad_attended[:, head_index * HEAD_DIM : (head_index + 1) * HEAD_DIM]
        query_pieces = []
        key_grad = jnp.zeros((group_rows, HEAD_DIM), jnp.float32)
        value_grad = jnp.zeros((group_rows, HEAD_DIM), jnp.float32)
        for block_index in range(block_count):
            first_row = block_index * block_rows
            last_row = first_row + block_rows
            scores = block_scores(head_index, first_row, last_row)
            row_probs = jnp.exp(scores - head_logs[head_index][first_row:last_row])
            grad_block = grad_heads[first_row:last_row]
            value_grad = value_grad.at[:last_row].add(
                contract_rows(row_probs.astype(jnp.bfloat16), grad_block)
            )
            grad_probs = contract_cols(grad_block, values[head_index, :last_row])
            row_delta = jnp.sum(grad_probs * row_probs, axis=1, keepdims=True)
            grad_score = (row_probs * (grad_probs - row_delta)).astype(jnp.bfloat16)
            query_pieces.append(
                jnp.dot(
                    grad_score, keys_all[head_index, :last_row], preferred_element_type=jnp.float32
                )
                * score_scale
            )
            key_grad = key_grad.at[:last_row].add(
                contract_rows(grad_score, queries[head_index, first_row:last_row]) * score_scale
            )
        query_grad = rotate_back(jnp.concatenate(query_pieces, axis=0), cos_table, sine_table)
        key_grad = rotate_back(key_grad, cos_table, sine_table)
        head_grads.append(jnp.stack([query_grad, key_grad, value_grad], axis=1))
    grad_qkv = (
        jnp.stack(head_grads, axis=1)
        .reshape(group_rows, heads_local * 3 * HEAD_DIM)
        .astype(jnp.bfloat16)
    )
    qkv_weight_grad = contract_rows(first_all, grad_qkv)
    qkv_bias_grad = jnp.sum(grad_qkv, axis=0, dtype=jnp.float32)
    first_grad = contract_cols(grad_qkv, qkv_weight)
    own_normed, own_inv_std = norm_stats(input_float)
    first_own_grad, second_own_grad = (
        lax.psum_scatter(first_grad, "mp", scatter_dimension=0, tiled=True),
        lax.psum_scatter(second_grad, "mp", scatter_dimension=0, tiled=True),
    )
    first_input_grad = norm_apply_back(own_normed, own_inv_std, first_own_grad * norm1_gain)
    second_input_grad = norm_apply_back(own_normed, own_inv_std, second_own_grad * norm2_gain)
    input_grad = cotangent.astype(jnp.float32) + first_input_grad + second_input_grad
    gain_one = jnp.sum(first_own_grad * own_normed, axis=0)
    shift_one = jnp.sum(first_own_grad, axis=0)
    gain_two = jnp.sum(second_own_grad * own_normed, axis=0)
    shift_two = jnp.sum(second_own_grad, axis=0)
    gain_one, shift_one, gain_two, shift_two = lax.psum(
        (gain_one, shift_one, gain_two, shift_two), "mp"
    )
    summed = lax.psum(
        (
            gain_one,
            shift_one,
            gain_two,
            shift_two,
            qkv_weight_grad,
            qkv_bias_grad,
            out_weight_grad,
            out_bias_grad,
            up_weight_grad,
            up_bias_grad,
            down_weight_grad,
        ),
        "dp",
    )
    return (
        layer_output,
        input_grad,
        summed[0],
        summed[1],
        summed[2],
        summed[3],
        summed[4],
        summed[5],
        summed[6],
        summed[7],
        summed[8],
        summed[9],
        summed[10],
        summed[7],
    )


def solution(mesh):
    in_specs = (
        P(("dp", "mp"), None),
        P("dp", None),
        P(),
        P(),
        P(),
        P(),
        P(None, "mp"),
        P("mp"),
        P("mp", None),
        P(),
        P(None, "mp"),
        P("mp"),
        P("mp", None),
        P(),
        P(("dp", "mp"), None),
    )
    out_specs = (
        P(("dp", "mp"), None),
        P(("dp", "mp"), None),
        P(),
        P(),
        P(),
        P(),
        P(None, "mp"),
        P("mp"),
        P("mp", None),
        P(),
        P(None, "mp"),
        P("mp"),
        P("mp", None),
        P(),
    )
    return jax.shard_map(
        per_device, mesh=mesh, in_specs=in_specs, out_specs=out_specs, check_vma=False
    )
```

profile of v0, /device:TPU:0, one launch (start us, length us, event | category | flops | bytes accessed | tf_op | source)
XLA Modules:
  0.0 1217.8 jit_solution(4417359608386559067)
XLA Ops:
  7.3 1.3 convert_reduce_fusion.3
  8.6 1.3 fusion.51
  10.0 2.6 fusion.38
  12.6 0.7 all-gather.8.cloned.1.call-update
  13.4 0.7 all-gather.4.cloned.1.call-update
  14.8 1.0 copy.84
  15.8 1.0 copy.83
  16.9 35.1 %all-gather.6.cloned.1.call-done = bf16[1024,2048]{1,0:T(8,128)(2,1)} async-done(((bf16[128,2048]{1,0:T(8,128)(2,1)}), bf16[1024,2048]{1,0:T(8,128)(2,1)}) %all-gather.6.cloned.1.call-update) | async-done | bytes 4194320 | tf_op jit(solution)/shard_map/all_gather | solution.py:119
  52.1 17.6 %fusion.2 = (bf16[1024,1024]{1,0:T(8,128)(2,1)}, f32[1024,1024]{1,0:T(8,128)}) fusion(f32[1024]{0:T(1024)S(1)} %copy-done.39, bf16[1024,2048]{1,0:T(8,128)(2,1)} %all-gather.6.cloned.1.call-done, bf16[2048,1024]{1,0:T(8,128)(2,1)} %param.49), kind=kOutput, calls=%fused_computation.6 | convolution fusion | flops 4364173312 | bytes 14684160 | tf_op jit(solution)/shard_map/dot_general | solution.py:169
  69.6 20.9 %all-gather.8.cloned.1.call-done = bf16[1024,2048]{1,0:T(8,128)(2,1)} async-done(((bf16[128,2048]{1,0:T(8,128)(2,1)}), bf16[1024,2048]{1,0:T(8,128)(2,1)}) %all-gather.8.cloned.1.call-update) | async-done | bytes 4194320 | tf_op jit(solution)/shard_map/all_gather | solution.py:179
  90.6 10.3 convert_reduce_fusion.1
  100.9 1.3 copy-done.44
  102.2 6.8 fusion.111
  109.0 10.0 reduce-scatter.6.cloned.1.call-start
  119.0 10.6 all-gather.4.cloned.1.call-done
  129.6 5.3 convolution_add_fusion.1
  136.2 0.8 fusion.105
  137.0 0.5 fusion.18
  137.6 2.1 copy-done.12
  139.7 0.6 copy-done.21
  140.3 1.3 convolution_convert_fusion
  142.5 0.6 multiply_reduce_fusion
  143.1 0.5 multiply_convert_fusion
  143.5 0.5 fusion.35
  144.8 0.8 fusion.107
  145.6 0.5 fusion.17
  147.1 0.6 multiply_reduce_fusion.1
  147.6 0.5 multiply_convert_fusion.1
  148.1 0.5 fusion.33
  149.9 0.4 convolution_multiply_fusion.8
  151.6 1.0 maximum_add_fusion
  153.5 0.6 fusion.36
  154.6 0.6 fusion.34
  155.3 1.5 convert_reduce_fusion.2
  156.9 2.6 copy.99
  159.4 7.1 fusion.110
  166.7 1.1 copy-done.7
  167.8 1.4 convolution_convert_fusion.1
  169.8 0.5 convolution_convert_fusion.3
  170.4 1.1 copy-done.5
  171.5 0.5 convolution_convert_fusion.4
  172.0 1.6 copy-done.36
  173.6 0.7 copy-done.42
  174.4 4.5 fusion.109
  178.9 4.5 convolution_add_fusion
  183.7 5.1 fusion.96
  188.8 5.4 fusion.112
  194.2 6.8 fusion.113
  201.0 6.7 fusion.114
  207.9 3.0 convert_reduce_fusion
  210.8 69.6 %reduce-scatter.6.cloned.1.call-done = f32[128,2048]{1,0:T(8,128)} async-done(((f32[1024,2048]{1,0:T(8,128)}), f32[128,2048]{1,0:T(8,128)}) %reduce-scatter.6.cloned.1.call-update) | async-done | bytes 1048592 | tf_op jit(solution)/shard_map/reduce_scatter | solution.py:233
  280.5 2.3 fusion.49
  282.8 22.9 %all-reduce.4 = (f32[2048]{0:T(1024)S(1)}, f32[2048]{0:T(1024)S(1)}, f32[2048]{0:T(1024)S(1)}, f32[2048]{0:T(1024)S(1)}) all-reduce(f32[2048]{0:T(1024)S(1)} %get-tuple-element.144, f32[2048]{0:T(1024)S(1)} %get-tuple-element.149, f32[2048]{0:T(1024)S(1)} %get-tuple-element.153, ...), channel_id=1, replica_groups=mesh['dp'=4,'mp'=8] {'mp'}, use_global_device_ids=true, to_apply=%region_25.26 | all-reduce | flops 8192 | bytes 65536 | tf_op jit(solution)/shard_map/psum | solution.py:243
  305.7 20.0 %all-reduce.5 = (f32[2048]{0:T(1024)}, f32[2048]{0:T(1024)}, f32[2048]{0:T(1024)}, f32[2048]{0:T(1024)}, f32[768]{0:T(1024)}, /*index=5*/f32[2048]{0:T(1024)S(1)}, f32[1024]{0:T(1024)}) all-reduce(f32[2048]{0:T(1024)S(1)} %get-tuple-element.154, f32[2048]{0:T(1024)S(1)} %get-tuple-element.155, ...), channel_id=1, replica_groups=mesh['dp'=4,'mp'=8] {'dp'}, use_global_device_ids=true, to_apply=%region_26.27 | all-reduce | flops 12032 | bytes 96256 | tf_op jit(solution)/shard_map/psum | solution.py:246
  325.7 29.6 %reduce-scatter.4.cloned.1.call-done = f32[128,2048]{1,0:T(8,128)} async-done(((f32[1024,2048]{1,0:T(8,128)}), f32[128,2048]{1,0:T(8,128)}) %reduce-scatter.4.cloned.1.call-update) | async-done | bytes 1048592 | tf_op jit(solution)/shard_map/reduce_scatter | solution.py:171
  355.3 3.8 fusion.45
  359.1 832.4 %all-reduce.9.cloned.1.call-done = (f32[2048,768]{1,0:T(8,128)}, f32[256,2048]{1,0:T(8,128)}, f32[2048,1024]{1,0:T(8,128)}, f32[1024,2048]{1,0:T(8,128)}) async-done(((f32[2048,768]{1,0:T(8,128)}, f32[256,2048]{1,0:T(8,128)}, f32[2048,1024]{1,0:T(8,128)}, f32[1024,2048]{1,0:T(8,128)}), (f32[2048,768]{1,0:T(8,128)}, f32[256,2048]{1,0:T(8,128)}, f32[2048,1024]{1,0:T(8,128)}, ...) | async-done | bytes 25165840 | tf_op jit(solution)/shard_map/psum | solution.py:246
  1191.5 0.6 copy.114
  1192.1 6.5 copy.115
  1198.7 1.3 copy.116
  1200.0 1.0 copy-done.11
  1201.0 4.3 copy.117
  1205.3 1.3 slice-done.1
  1206.6 3.9 copy.118
  (161 shorter events, 10.0 us)
Async XLA Ops:
  7.2 122.5 %copy-start = (bf16[2048,768]{1,0:T(8,128)(2,1)S(1)}, bf16[2048,768]{1,0:T(8,128)(2,1)}, u32[]{:S(2)}) copy-start(bf16[2048,768]{1,0:T(8,128)(2,1)} %param.45) | copy-start | bytes 9437188
  7.2 7.0 copy-start.41
  7.2 44.9 %copy-start.39 = (f32[1024]{0:T(1024)S(1)}, f32[1024]{0:T(1024)}, u32[]{:S(2)}) copy-start(f32[1024]{0:T(1024)} %param.50) | copy-start | bytes 12292
  7.2 44.8 %all-gather.6.cloned.1.call-start = ((), (), s32[]{:S(2)}) async-start(), calls=%async_computation.4 | async-start | bytes 4718592 | tf_op jit(solution)/shard_map/all_gather | solution.py:119
  8.6 1.4 copy-start.30
  10.0 2.6 copy-start.32
  12.6 78.0 %all-gather.8.cloned.1.call-start = ((), (), s32[]{:S(2)}) async-start(), calls=%async_computation.6 | async-start | bytes 4718592 | tf_op jit(solution)/shard_map/all_gather | solution.py:179
  13.3 116.3 %all-gather.4.cloned.1.call-start = ((), (), s32[]{:S(2)}) async-start(), calls=%async_computation.3 | async-start | bytes 4718592 | tf_op jit(solution)/shard_map/all_gather | solution.py:118
  14.1 196.8 %reduce-scatter.8.cloned.1.call-start = ((), (), s32[]{:S(2)}) async-start(), calls=%async_computation.8 | async-start | bytes 9437184 | tf_op jit(solution)/shard_map/reduce_scatter | solution.py:234
  90.6 11.7 copy-start.35
  100.9 1.4 copy-start.44
  109.0 20.7 %copy-start.40 = (f32[768]{0:T(1024)S(1)}, f32[768]{0:T(1024)}, u32[]{:S(2)}) copy-start(f32[768]{0:T(1024)} %param.46) | copy-start | bytes 9220
  109.0 171.4 %reduce-scatter.6.cloned.1.call-start = ((), (), s32[]{:S(2)}) async-start(), calls=%async_computation.7 | async-start | bytes 9437184 | tf_op jit(solution)/shard_map/reduce_scatter | solution.py:233
  136.0 17.2 %copy-start.6 = (f32[512,512]{0,1:T(8,128)}, f32[512,512]{0,1:T(8,128)S(1)}, u32[]{:S(2)}) copy-start(f32[512,512]{0,1:T(8,128)S(1)} %get-tuple-element.206) | copy-start | bytes 3145732
  136.0 3.6 copy-start.12
  136.0 4.2 copy-start.21
  137.0 16.5 %copy-start.2 = (f32[512,1024]{1,0:T(8,128)}, f32[512,1024]{1,0:T(8,128)S(1)}, u32[]{:S(2)}) copy-start(f32[512,1024]{1,0:T(8,128)S(1)} %get-tuple-element.204) | copy-start | bytes 6291460
  140.3 6.8 copy-start.14
  144.6 9.6 copy-start.8
  145.6 9.0 copy-start.4
  146.1 1.6 copy-start.28
  148.1 2.3 copy-start.16
  150.5 1.1 copy-start.19
  166.6 1.2 copy-start.7
  166.6 3.2 copy-start.3
  166.6 188.7 %reduce-scatter.4.cloned.1.call-start = ((), (), s32[]{:S(2)}) async-start(), calls=%async_computation.5 | async-start | bytes 9437184 | tf_op jit(solution)/shard_map/reduce_scatter | solution.py:171
  167.8 1.5 copy-start.9
  167.8 1.6 copy-start.15
  169.8 1.6 copy-start.5
  169.8 1.6 copy-start.29
  171.4 2.2 copy-start.36
  171.4 2.9 copy-start.42
  174.4 4.5 copy-start.22
  183.5 5.3 copy-start.20
  183.5 1008.1 %all-reduce.9.cloned.1.call-start = ((), (), s32[]{:S(2)}) async-start(), calls=%async_computation.9 | async-start | bytes 50331648 | tf_op jit(solution)/shard_map/psum | solution.py:246
  183.7 5.1 copy-start.38
  188.8 5.4 copy-start.37
  188.8 5.4 copy-start.45
  194.2 6.8 copy-start.13
  194.2 6.8 copy-start.43
  207.7 72.7 %copy-start.10 = (bf16[128,2048]{1,0:T(8,128)(2,1)S(1)}, bf16[128,2048]{1,0:T(8,128)(2,1)}, u32[]{:S(2)}) copy-start(bf16[128,2048]{1,0:T(8,128)(2,1)} %param.39) | copy-start | bytes 1572868
  207.7 72.7 %copy-start.23 = (f32[2048]{0:T(1024)S(1)}, f32[2048]{0:T(1024)}, u32[]{:S(2)}) copy-start(f32[2048]{0:T(1024)} %param.41) | copy-start | bytes 24580
  207.8 72.7 %copy-start.24 = (f32[2048]{0:T(1024)S(1)}, f32[2048]{0:T(1024)}, u32[]{:S(2)}) copy-start(f32[2048]{0:T(1024)} %param.43) | copy-start | bytes 24580
  207.8 72.7 %copy-start.31 = (f32[128]{0:T(128)S(1)}, f32[128]{0:T(128)}, u32[]{:S(2)}) copy-start(f32[128]{0:T(128)} %copy-done.30) | copy-start | bytes 1540
  207.8 72.7 %copy-start.33 = (f32[128]{0:T(128)S(1)}, f32[128]{0:T(128)}, u32[]{:S(2)}) copy-start(f32[128]{0:T(128)} %copy-done.32) | copy-start | bytes 1540
  207.8 97.9 %copy-start.34 = (f32[1024]{0:T(1024)S(1)}, f32[1024]{0:T(1024)}, u32[]{:S(2)}) copy-start(f32[1024]{0:T(1024)} %get-tuple-element.221) | copy-start | bytes 12292
  207.8 147.5 %copy-start.17 = (bf16[128,2048]{1,0:T(8,128)(2,1)S(1)}, bf16[128,2048]{1,0:T(8,128)(2,1)}, u32[]{:S(2)}) copy-start(bf16[128,2048]{1,0:T(8,128)(2,1)} %param.53) | copy-start | bytes 1572868
  207.8 147.5 %copy-start.25 = (f32[2048]{0:T(1024)S(1)}, f32[2048]{0:T(1024)}, u32[]{:S(2)}) copy-start(f32[2048]{0:T(1024)} %param.52) | copy-start | bytes 24580
  207.8 147.5 %copy-start.26 = (f32[2048]{0:T(1024)S(1)}, f32[2048]{0:T(1024)}, u32[]{:S(2)}) copy-start(f32[2048]{0:T(1024)} %param.48) | copy-start | bytes 24580
  325.6 873.1 %copy-start.27 = (f32[2048]{0:T(1024)}, f32[2048]{0:T(1024)S(1)}, u32[]{:S(2)}) copy-start(f32[2048]{0:T(1024)S(1)} %get-tuple-element.264) | copy-start | bytes 24580
  1192.1 6.6 copy-start.18
  1192.1 8.9 copy-start.11
  1198.7 6.6 slice-start
  1201.0 5.6 slice-start.1
  1206.6 4.2 copy-start.1
Sparse Core Ops, SparseCore 0:
  12.7 39.2 all-gather.5
  53.9 36.5 all-gather.7
  93.0 36.5 all-gather.3
  133.5 71.4 reduce-scatter.7
  208.9 71.4 reduce-scatter.5
  283.8 71.4 reduce-scatter.3
  358.8 832.7 all-reduce.8
where the time goes:
time: 1230 us; the launch traced here: 1220 us
  waiting for transfers between devices  1000 us (81%)
  matrix products  93.6 us (8%)
  blocking collectives  42.9 us (3%)
  local copies, waits for them, and re-layouts  33.7 us (3%)
  other arithmetic  22.3 us (2%)
  between operations  15.1 us (1%)
    psum x1, waiting for transfers between devices, per_device(): lax.psum((gain_one, shift_one, gain_two, shift_two, qkv_weight_grad, qkv_...  832 us
    reduce_scatter x1, waiting for transfers between devices, per_device(): lax.psum_scatter(first_grad, 'mp', scatter_dimension=0, tiled=True)  69.6 us
    all_gather x1, waiting for transfers between devices, per_device(): lax.all_gather(second_own, 'mp', axis=0, tiled=True)  35.1 us
    dot_general x12, matrix products, contract_cols(): lax.dot_general(left, right, (((1,), (1,)), ((), ())), preferred_element_...  29.8 us
    reduce_scatter x1, waiting for transfers between devices, per_device(): lax.psum_scatter(jnp.dot(attended, out_weight, preferred_element_type=jnp...  29.6 us
    unnamed x101, local copies, waits for them, and re-layouts  28.5 us
    dot_general x12, matrix products, contract_rows(): lax.dot_general(left, right, (((0,), (0,)), ((), ())), preferred_element_...  27.5 us
  transfers between devices with their start and end apart: 7, of which 6 were waited for; matrix products, arithmetic and copies ran while one was open for 10% of the time, Pallas kernels for 0%

commit v1 on v0

v1 whole, which is shorter than its diff:
```python
import functools

import jax
import jax.numpy as jnp
from jax import lax
from jax.experimental import pallas as pl
from jax.experimental.pallas import tpu as pltpu
from jax.sharding import PartitionSpec as P

HEAD_DIM = 128
ROTARY = 32

norm_eps = 1e-05
masked_score = -1e30
inv_root_two = 0.7071067811865476
inv_root_tau = 0.3989422804014327
vmem_bytes = 60 << 20
gather_bytes = 128 << 20
bf16 = jnp.bfloat16
f32 = jnp.float32


def dot_plain(left, right):
    return jnp.dot(left, right, preferred_element_type=f32)


def contract_rows(left, right):
    return lax.dot_general(left, right, (((0,), (0,)), ((), ())), preferred_element_type=f32)


def contract_cols(left, right):
    return lax.dot_general(left, right, (((1,), (1,)), ((), ())), preferred_element_type=f32)


def swap(value, axis, count, bit):
    return lax.ppermute(value, axis, [(i, i ^ bit) for i in range(count)])


def turn(value, axis, count, step):
    return lax.ppermute(value, axis, [(i, (i + step) % count) for i in range(count)])


def chip_bits(count):
    return [1 << i for i in range(1, count.bit_length() - 1)]


def after(value, *earlier):
    return lax.optimization_barrier((value, *earlier))[0]


def halves(pair):
    rows = pair.shape[0] // 2
    return pair[:rows], pair[rows:]


class Spread:
    def __init__(self, arrays, a, b, names):
        self.arrays, self.a, self.b, self.names = arrays, a, b, names


def spread_sides(pair, count):
    return swap(pair, "mp", count, 2), swap(pair, "mp", count, 4)


def spread_corner(side_x, side_y, count):
    return swap(halves(side_x)[0], "mp", count, 4), swap(halves(side_y)[1], "mp", count, 2)


def spread_four(pair, sides, corner, count):
    rows = pair.shape[0] // 2
    arrays = [pair, *sides, *corner]
    arrays = arrays + [swap(array, "mp", count, 1) for array in arrays]
    a, b = {}, {}
    for core in range(2):
        base = 5 * core
        for i, name in enumerate((0, 2, 4)):
            a[name + core] = (base + i, 0)
            b[name + core] = (base + i, rows)
        a[6 + core] = (base + 3, 0)
        b[6 + core] = (base + 4, 0)
    return Spread(arrays, a, b, (0, 2, 4, 6, 1, 3, 5, 7))


def spread_any(pair, count):
    rows = pair.shape[0] // 2
    held, names = pair.reshape(1, 2, rows, -1), [0]
    for bit in chip_bits(count) + [1]:
        held = jnp.concatenate([held, swap(held, "mp", count, bit)], axis=0)
        names = names + [n ^ bit for n in names]
    arrays = [held.reshape(2 * rows * count, -1)]
    a = {n: (0, 2 * rows * i) for i, n in enumerate(names)}
    b = {n: (0, 2 * rows * i + rows) for i, n in enumerate(names)}
    return Spread(arrays, a, b, tuple(names))


def scatter_group(near, far, names, count, rows, rising):
    bits = chip_bits(count)
    came = swap(far, "mp", count, 1)
    names = names[: len(names) // 2]
    blocks = {n: near[i * rows : (i + 1) * rows] for i, n in enumerate(names)}
    adds = {n: came[i * rows : (i + 1) * rows] for i, n in enumerate(names)}
    for bit in bits if rising else bits[::-1]:
        stay = [n for n in blocks if not n & bit]

        def total(n):
            return (blocks[n].astype(f32) + adds[n].astype(f32)).astype(bf16)

        sent = jnp.concatenate([total(n | bit) for n in stay], axis=0)
        came = swap(sent, "mp", count, bit)
        blocks = {n: total(n) for n in stay}
        adds = {n: came[i * rows : (i + 1) * rows] for i, n in enumerate(stay)}
    return blocks[0].astype(f32) + adds[0].astype(f32)


def call(body, name, flops, moved, **kwargs):
    return pl.pallas_call(
        body,
        name=name,
        compiler_params=pltpu.CompilerParams(vmem_limit_bytes=vmem_bytes),
        cost_estimate=pl.CostEstimate(flops=flops, bytes_accessed=moved, transcendentals=0),
        **kwargs,
    )


def block_copies(spread, which, refs, buffer, sems, rows, block):
    copies = []
    for i, name in enumerate(spread.names):
        array, first = getattr(spread, which)[name]
        copies.append(
            pltpu.make_async_copy(
                refs[array].at[first : first + rows, :],
                buffer.at[i * rows : (i + 1) * rows, :],
                sems.at[i],
            )
        )
    per = block // rows
    return [copies[i : i + per] for i in range(0, len(copies), per)]


def out_copies(buffer, ref, sems, block):
    count = buffer.shape[0] // block
    return [
        pltpu.make_async_copy(
            buffer.at[i * block : (i + 1) * block, :],
            ref.at[i * block : (i + 1) * block, :],
            sems.at[i],
        )
        for i in range(count)
    ]


def entry_body(*refs, spread, rows, block):
    count = len(spread.arrays)
    arrays = refs[:count]
    (gain1, bias1, gain2, bias2, qkv_ref, out_weight_ref) = refs[count : count + 6]
    (one_ref, two_ref, hat_ref, raw_ref, grad_ref, cot_ref) = refs[count + 6 : count + 12]
    x_buf, c_buf, sem_x, sem_c, sem_out = refs[count + 12 :]
    step = pl.program_id(0)
    x_copies = block_copies(spread, "a", arrays, x_buf, sem_x, rows, block)
    c_copies = block_copies(spread, "b", arrays, c_buf, sem_c, rows, block)
    outs = out_copies(c_buf, cot_ref, sem_out, block)

    @pl.when(step == 0)
    def _():
        for x_list, c_list in zip(x_copies, c_copies):
            for copy in x_list + c_list:
                copy.start()

    for i in range(len(outs)):

        @pl.when(step == i)
        def _(i=i):
            for copy in x_copies[i] + c_copies[i]:
                copy.wait()
            outs[i].start()

    here = pl.ds(pl.multiple_of(step * block, block), block)
    values = x_buf[here, :].astype(f32)
    centred = values - jnp.mean(values, axis=1, keepdims=True)
    hat = centred * lax.rsqrt(jnp.mean(centred * centred, axis=1, keepdims=True) + norm_eps)
    hat_ref[...] = hat.astype(bf16)
    one_ref[...] = (hat * gain1[...] + bias1[...]).astype(bf16)
    two_ref[...] = (hat * gain2[...] + bias2[...]).astype(bf16)
    raw_ref[...] = dot_plain(one_ref[...], qkv_ref[...])
    grad_ref[...] = contract_cols(c_buf[here, :], out_weight_ref[...]).astype(bf16)

    @pl.when(step == len(outs) - 1)
    def _():
        for copy in outs:
            copy.wait()


def entry(spread, rows, gains, qkv_weight, out_weight):
    group_rows = rows * len(spread.names)
    width, deep = qkv_weight.shape
    units = out_weight.shape[0]
    block = min(256, group_rows)
    steps = group_rows // block
    blocks = len(spread.names)
    once = pl.Buffered(1)
    full = pl.BlockSpec((block, width), lambda i: (i, 0))
    row = pl.BlockSpec((1, width), lambda i: (0, 0))
    anywhere = pl.BlockSpec(memory_space=pl.ANY)
    wide = jax.ShapeDtypeStruct((group_rows, width), bf16)
    return call(
        functools.partial(entry_body, spread=spread, rows=rows, block=block),
        "entry",
        2 * group_rows * width * (deep + units),
        12 * group_rows * width,
        grid=(steps,),
        in_specs=[anywhere] * len(spread.arrays)
        + [row] * 4
        + [
            pl.BlockSpec(qkv_weight.shape, lambda i: (0, 0), pipeline_mode=once),
            pl.BlockSpec(out_weight.shape, lambda i: (0, 0), pipeline_mode=once),
        ],
        out_specs=[
            full,
            full,
            full,
            pl.BlockSpec((block, deep), lambda i: (i, 0)),
            pl.BlockSpec((block, units), lambda i: (i, 0)),
            anywhere,
        ],
        out_shape=[
            wide,
            wide,
            wide,
            jax.ShapeDtypeStruct((group_rows, deep), f32),
            jax.ShapeDtypeStruct((group_rows, units), bf16),
            wide,
        ],
        scratch_shapes=[
            pltpu.VMEM((group_rows, width), bf16),
            pltpu.VMEM((group_rows, width), bf16),
            pltpu.SemaphoreType.DMA((blocks,)),
            pltpu.SemaphoreType.DMA((blocks,)),
            pltpu.SemaphoreType.DMA((steps,)),
        ],
    )(*spread.arrays, *gains, qkv_weight, out_weight)


def mlp_body(*refs, spread, rows, block, tile, keep):
    count = len(spread.arrays)
    arrays = refs[:count]
    up_ref, shift_ref, down_ref, hidden_ref, grad_ref, sum_ref = refs[count : count + 6]
    rest = refs[count + 6 :]
    if keep:
        rows_ref, cot_ref = rest[:2]
        rest = rest[2:]
    x_buf, c_buf, u_buf, d_buf, sem_x, sem_c, sem_u, sem_d, sem_ox, sem_oc = rest
    step = pl.program_id(0)
    units = u_buf.shape[1]
    x_copies = block_copies(spread, "a", arrays, x_buf, sem_x, rows, block)
    c_copies = block_copies(spread, "b", arrays, c_buf, sem_c, rows, block)
    tiles = [slice(i, i + tile) for i in range(0, units, tile)]
    u_copies = [
        pltpu.make_async_copy(up_ref.at[:, t], u_buf.at[:, t], sem_u.at[i])
        for i, t in enumerate(tiles)
    ]
    d_copies = [
        pltpu.make_async_copy(down_ref.at[t, :], d_buf.at[t, :], sem_d.at[i])
        for i, t in enumerate(tiles)
    ]
    outs = []
    if keep:
        outs = list(
            zip(
                out_copies(x_buf, rows_ref, sem_ox, block),
                out_copies(c_buf, cot_ref, sem_oc, block),
            )
        )

    @pl.when(step == 0)
    def _():
        for copy in x_copies[0] + u_copies[:1] + c_copies[0] + d_copies[:1]:
            copy.start()
        for pair in zip(u_copies[1:], d_copies[1:]):
            for copy in pair:
                copy.start()
        for x_list, c_list in zip(x_copies[1:], c_copies[1:]):
            for copy in x_list + c_list:
                copy.start()
        sum_ref[...] = jnp.zeros_like(sum_ref)

    for i in range(len(x_copies)):

        @pl.when(step == i)
        def _(i=i):
            for copy in x_copies[i] + c_copies[i]:
                copy.wait()
            if keep:
                outs[i][0].start()
                outs[i][1].start()

    here = pl.ds(pl.multiple_of(step * block, block), block)
    for i, part in enumerate(tiles):

        @pl.when(step == 0)
        def _(i=i):
            u_copies[i].wait()
            d_copies[i].wait()

        gate = dot_plain(x_buf[here, :], u_buf[:, part]) + shift_ref[:, part]
        grad_hidden = contract_cols(c_buf[here, :], d_buf[part, :])
        below = 0.5 * (1.0 + lax.erf(gate * inv_root_two))
        hidden_ref[:, part] = (gate * below).astype(bf16)
        slope = below + gate * jnp.exp(-0.5 * gate * gate) * inv_root_tau
        grad = (grad_hidden * slope).astype(bf16)
        grad_ref[:, part] = grad
        sum_ref[:, part] += jnp.sum(grad.astype(f32), axis=0, keepdims=True)

    if keep:

        @pl.when(step == len(x_copies) - 1)
        def _():
            for pair in outs:
                for copy in pair:
                    copy.wait()


def mlp(spread, rows, up_weight, up_bias, down_weight, keep):
    width, units = up_weight.shape
    group_rows = rows * len(spread.names)
    block = min(512, group_rows)
    tile = min(512, units)
    steps, tiles, blocks = group_rows // block, units // tile, len(spread.names)
    anywhere = pl.BlockSpec(memory_space=pl.ANY)
    part = pl.BlockSpec((block, units), lambda i: (i, 0))
    low = jax.ShapeDtypeStruct((group_rows, units), bf16)
    wide = jax.ShapeDtypeStruct((group_rows, width), bf16)
    dma = pltpu.SemaphoreType.DMA
    return call(
        functools.partial(mlp_body, spread=spread, rows=rows, block=block, tile=tile, keep=keep),
        "mlp",
        4 * group_rows * width * units,
        8 * group_rows * width + 4 * width * units,
        grid=(steps,),
        in_specs=[anywhere] * len(spread.arrays)
        + [anywhere, pl.BlockSpec((1, units), lambda i: (0, 0)), anywhere],
        out_specs=[part, part, pl.BlockSpec((1, units), lambda i: (0, 0))]
        + [anywhere] * (2 * keep),
        out_shape=[low, low, jax.ShapeDtypeStruct((1, units), f32)] + [wide] * (2 * keep),
        scratch_shapes=[
            pltpu.VMEM((group_rows, width), bf16),
            pltpu.VMEM((group_rows, width), bf16),
            pltpu.VMEM((width, units), bf16),
            pltpu.VMEM((units, width), bf16),
            dma((blocks,)),
            dma((blocks,)),
            dma((tiles,)),
            dma((tiles,)),
            dma((steps,)),
            dma((steps,)),
        ],
    )(*spread.arrays, up_weight, up_bias, down_weight)


def weight_body(*refs, pieces):
    out_ref = refs[2 * pieces]
    total = contract_rows(refs[0][...], refs[pieces][...])
    for piece in range(1, pieces):
        total = total + contract_rows(refs[piece][...], refs[pieces + piece][...])
    out_ref[...] = total.astype(out_ref.dtype)


def weight_product(lefts, rights, tile_left, kind):
    wide, deep = lefts[0].shape[1], rights[0].shape[1]
    tile = min(512, wide if tile_left else deep)
    once = pl.Buffered(1)

    def spec(piece, tiled):
        if tiled:
            return pl.BlockSpec((piece.shape[0], tile), lambda i: (0, i))
        return pl.BlockSpec(piece.shape, lambda i: (0, 0), pipeline_mode=once)

    rows = sum(piece.shape[0] for piece in lefts)
    return call(
        functools.partial(weight_body, pieces=len(lefts)),
        "weight_product",
        2 * rows * wide * deep,
        2 * rows * (wide + deep) + 4 * wide * deep,
        grid=((wide if tile_left else deep) // tile,),
        in_specs=[spec(p, tile_left) for p in lefts] + [spec(p, not tile_left) for p in rights],
        out_specs=(
            pl.BlockSpec((tile, deep), lambda i: (i, 0))
            if tile_left
            else pl.BlockSpec((wide, tile), lambda i: (0, i))
        ),
        out_shape=jax.ShapeDtypeStruct((wide, deep), kind),
    )(*lefts, *rights)


def branch_body(attended_ref, hidden_ref, out_ref, down_ref, near_ref, far_ref):
    middle = near_ref.shape[0]
    total = dot_plain(attended_ref[...], out_ref[...]) + dot_plain(hidden_ref[...], down_ref[...])
    near_ref[...] = total[:middle].astype(bf16)
    far_ref[...] = total[middle:].astype(bf16)


def branch_sum(attended, hidden, out_weight, down_weight):
    group_rows = attended.shape[0]
    width = out_weight.shape[1]
    tile = min(512, width)
    once = pl.Buffered(1)
    half = pl.BlockSpec((group_rows // 2, tile), lambda i: (0, i))
    depth = attended.shape[1] + hidden.shape[1]
    return call(
        branch_body,
        "branch_sum",
        2 * group_rows * width * depth,
        2 * (group_rows * depth + width * depth + group_rows * width),
        grid=(width // tile,),
        in_specs=[
            pl.BlockSpec(attended.shape, lambda i: (0, 0), pipeline_mode=once),
            pl.BlockSpec(hidden.shape, lambda i: (0, 0), pipeline_mode=once),
            pl.BlockSpec((out_weight.shape[0], tile), lambda i: (0, i)),
            pl.BlockSpec((down_weight.shape[0], tile), lambda i: (0, i)),
        ],
        out_specs=[half, half],
        out_shape=[jax.ShapeDtypeStruct((group_rows // 2, width), bf16)] * 2,
    )(attended, hidden, out_weight, down_weight)


def input_body(
    qkv_grad_ref, gate_grad_ref, qkv_ref, up_ref, gain1, gain2, hat_ref, near_ref, far_ref, sum_ref
):
    middle = near_ref.shape[0]
    hat = hat_ref[...].astype(f32)
    first = contract_cols(qkv_grad_ref[...], qkv_ref[...])
    second = contract_cols(gate_grad_ref[...], up_ref[...])
    both = first * gain1[...] + second * gain2[...]
    near_ref[...] = both[:middle].astype(bf16)
    far_ref[...] = both[middle:].astype(bf16)
    sum_ref[0:1, :] = jnp.sum(first * hat, axis=0, keepdims=True)
    sum_ref[1:2, :] = jnp.sum(first, axis=0, keepdims=True)
    sum_ref[2:3, :] = jnp.sum(second * hat, axis=0, keepdims=True)
    sum_ref[3:4, :] = jnp.sum(second, axis=0, keepdims=True)


def input_sums(grad_qkv, grad_gate, qkv_weight, up_weight, gain1, gain2, hat):
    group_rows = grad_qkv.shape[0]
    width = qkv_weight.shape[0]
    tile = min(256, width)
    once = pl.Buffered(1)
    half = pl.BlockSpec((group_rows // 2, tile), lambda i: (0, i))
    row = pl.BlockSpec((1, tile), lambda i: (0, i))
    depth = grad_qkv.shape[1] + grad_gate.shape[1]
    return call(
        input_body,
        "input_sums",
        2 * group_rows * width * depth,
        2 * (group_rows * depth + width * depth + 2 * group_rows * width),
        grid=(width // tile,),
        in_specs=[
            pl.BlockSpec(grad_qkv.shape, lambda i: (0, 0), pipeline_mode=once),
            pl.BlockSpec(grad_gate.shape, lambda i: (0, 0), pipeline_mode=once),
            pl.BlockSpec((tile, qkv_weight.shape[1]), lambda i: (i, 0)),
            pl.BlockSpec((tile, up_weight.shape[1]), lambda i: (i, 0)),
            row,
            row,
            pl.BlockSpec((group_rows, tile), lambda i: (0, i)),
        ],
        out_specs=[half, half, pl.BlockSpec((4, tile), lambda i: (0, i))],
        out_shape=[jax.ShapeDtypeStruct((group_rows // 2, width), bf16)] * 2
        + [jax.ShapeDtypeStruct((4, width), f32)],
    )(grad_qkv, grad_gate, qkv_weight, up_weight, gain1, gain2, hat)


def attention_body(
    own_ref,
    starts_ref,
    raw_ref,
    bias_ref,
    cos_ref,
    sine_ref,
    slope_in_ref,
    attended_ref,
    grad_qkv_ref,
    bias_grad_ref,
    query_ref,
    key_ref,
    value_ref,
    slope_ref,
    query_sum_ref,
    key_sum_ref,
    value_sum_ref,
    *,
    rows,
    names,
    block_rows,
    longest,
):
    own = own_ref[0]
    group_rows = rows * len(names)
    lane = lax.broadcasted_iota(jnp.int32, (rows, HEAD_DIM), 1)
    half = ROTARY // 2
    scale = HEAD_DIM ** (-0.5)

    def turned(u):
        return jnp.where(lane < half, pltpu.roll(u, HEAD_DIM - half, 1), pltpu.roll(u, half, 1))

    def far_rows(name):
        return pl.ds(pl.multiple_of((own ^ name) * rows, rows), rows)

    for i, name in enumerate(names):
        near = slice(i * rows, (i + 1) * rows)
        far = far_rows(name)
        raw = raw_ref[near, :] + bias_ref[...]
        cos_table = cos_ref[near, :]
        sine_table = sine_ref[near, :]
        query = raw[:, :HEAD_DIM]
        key = raw[:, HEAD_DIM : 2 * HEAD_DIM]
        query_ref[far, :] = (query * cos_table + turned(query) * sine_table).astype(bf16)
        key_ref[far, :] = (key * cos_table + turned(key) * sine_table).astype(bf16)
        value_ref[far, :] = raw[:, 2 * HEAD_DIM :].astype(bf16)
        slope_ref[far, :] = slope_in_ref[near, :]
    key_sum_ref[...] = jnp.zeros_like(key_sum_ref)
    value_sum_ref[...] = jnp.zeros_like(value_sum_ref)
    for first in range(0, group_rows, block_rows):
        last = first + block_rows
        low = max(0, (first - longest + 1) // 128 * 128)
        query = query_ref[first:last, :]
        keys = key_ref[low:last, :]
        values = value_ref[low:last, :]
        slope = slope_ref[first:last, :]
        scores = contract_cols(query, keys) * scale
        row = first + lax.broadcasted_iota(jnp.int32, (block_rows, 1), 0)
        begin = jnp.zeros((block_rows, 1), jnp.int32)
        for slot in range(starts_ref.shape[0]):
            begin = jnp.where(starts_ref[slot] <= row, starts_ref[slot], begin)
        column = low + lax.broadcasted_iota(jnp.int32, scores.shape, 1)
        scores = jnp.where((column >= begin) & (column <= row), scores, masked_score)
        peak = jnp.max(scores, axis=1, keepdims=True)
        raised = jnp.exp(scores - peak)
        probs = raised * (1.0 / jnp.sum(raised, axis=1, keepdims=True))
        probs_low = probs.astype(bf16)
        query_ref[first:last, :] = dot_plain(probs_low, values).astype(bf16)
        grad_probs = contract_cols(slope, values)
        delta = jnp.sum(grad_probs * probs, axis=1, keepdims=True)
        grad_score = (probs * (grad_probs - delta)).astype(bf16)
        query_sum_ref[first:last, :] = dot_plain(grad_score, keys) * scale
        key_sum_ref[low:last, :] += contract_rows(grad_score, query) * scale
        value_sum_ref[low:last, :] += contract_rows(probs_low, slope)
    bias_grad = jnp.zeros(bias_grad_ref.shape, f32)
    for i, name in enumerate(names):
        near = slice(i * rows, (i + 1) * rows)
        far = far_rows(name)
        cos_table = cos_ref[near, :]
        sine_table = sine_ref[near, :]
        query_grad = query_sum_ref[far, :]
        key_grad = key_sum_ref[far, :]
        grads = jnp.concatenate(
            [
                query_grad * cos_table - turned(query_grad) * sine_table,
                key_grad * cos_table - turned(key_grad) * sine_table,
                value_sum_ref[far, :],
            ],
            axis=1,
        ).astype(bf16)
        grad_qkv_ref[near, :] = grads
        bias_grad = bias_grad + jnp.sum(grads.astype(f32), axis=0, keepdims=True)
        attended_ref[near, :] = query_ref[far, :]
    bias_grad_ref[...] = bias_grad


def attention(own, starts, raw, bias, cos_table, sine_table, slope, rows, names):
    group_rows, width = raw.shape
    part = 3 * HEAD_DIM
    heads = width // part
    whole = pl.BlockSpec((group_rows, HEAD_DIM), lambda h: (0, 0))
    scalars = pl.BlockSpec(memory_space=pltpu.SMEM)
    low = pltpu.VMEM((group_rows, HEAD_DIM), bf16)
    wide = pltpu.VMEM((group_rows, HEAD_DIM), f32)
    longest = group_rows // 2
    return pl.pallas_call(
        functools.partial(
            attention_body,
            rows=rows,
            names=names,
            block_rows=min(256, group_rows),
            longest=longest,
        ),
        grid=(heads,),
        in_specs=[
            scalars,
            scalars,
            pl.BlockSpec((group_rows, part), lambda h: (0, h)),
            pl.BlockSpec((1, part), lambda h: (0, h)),
            whole,
            whole,
            pl.BlockSpec((group_rows, HEAD_DIM), lambda h: (0, h)),
        ],
        out_specs=[
            pl.BlockSpec((group_rows, HEAD_DIM), lambda h: (0, h)),
            pl.BlockSpec((group_rows, part), lambda h: (0, h)),
            pl.BlockSpec((1, part), lambda h: (0, h)),
        ],
        out_shape=[
            jax.ShapeDtypeStruct((group_rows, heads * HEAD_DIM), bf16),
            jax.ShapeDtypeStruct((group_rows, width), bf16),
            jax.ShapeDtypeStruct((1, width), f32),
        ],
        scratch_shapes=[low, low, low, low, wide, wide, wide],
        compiler_params=pltpu.CompilerParams(vmem_limit_bytes=vmem_bytes),
        cost_estimate=pl.CostEstimate(
            flops=12 * heads * group_rows * longest * HEAD_DIM,
            bytes_accessed=12 * group_rows * width,
            transcendentals=heads * group_rows * longest,
        ),
        name="attention",
    )(own, starts, raw, bias, cos_table, sine_table, slope)


def rotary_tables(position):
    half_rot = ROTARY // 2
    frequency = 10000.0 ** (-2.0 * jnp.arange(half_rot, dtype=f32) / ROTARY)
    angles = position.astype(f32)[:, None] * frequency[None, :]
    cos_half = jnp.cos(angles)
    sine_half = jnp.sin(angles)
    rest = (position.shape[0], HEAD_DIM - ROTARY)
    return (
        jnp.concatenate([cos_half, cos_half, jnp.ones(rest, f32)], axis=1),
        jnp.concatenate([-sine_half, sine_half, jnp.zeros(rest, f32)], axis=1),
    )


def per_device(
    layer_input,
    lengths,
    norm1_gain,
    norm1_bias,
    norm2_gain,
    norm2_bias,
    qkv_weight,
    qkv_bias,
    out_weight,
    out_bias,
    up_weight,
    up_bias,
    down_weight,
    down_bias,
    cotangent,
):
    dp = lax.axis_size("dp")
    mp = lax.axis_size("mp")
    own = lax.axis_index("mp")
    rows = layer_input.shape[0]
    group_rows = rows * mp
    four = mp == 8
    up_row = up_bias[None, :]
    width = layer_input.shape[1]

    pair = jnp.concatenate([layer_input, cotangent], axis=0)
    if four:
        sides = spread_sides(pair, mp)
    input_float = layer_input.astype(f32)
    centred = input_float - jnp.mean(input_float, axis=-1, keepdims=True)
    inv_std = lax.rsqrt(jnp.mean(centred * centred, axis=-1, keepdims=True) + norm_eps)
    xhat = centred * inv_std
    second_own = (xhat * norm2_gain + norm2_bias).astype(bf16)
    shared = jnp.concatenate([second_own, cotangent], axis=0)
    ring = []
    ahead = behind = shared
    lean = dp * group_rows * (width + up_weight.shape[1]) * 4 > gather_bytes
    for step in range(1, 0 if lean else dp // 2 + 1):
        if four and step == 2:
            ahead = after(ahead, sides[0])
        ahead = turn(ahead, "dp", dp, 1)
        ring.append(ahead)
        if 2 * step < dp:
            behind = turn(behind, "dp", dp, -1)
            ring.append(behind)
    if four:
        corner = spread_corner(*sides, mp)
        spread = spread_four(pair, sides, corner, mp)
    else:
        spread = spread_any(pair, mp)
    names = spread.names

    seq_ends = jnp.cumsum(lengths[0])
    seq_starts = seq_ends - lengths[0]
    places = (
        (own ^ jnp.array(names, jnp.int32))[:, None] * rows
        + jnp.arange(rows, dtype=jnp.int32)[None, :]
    ).reshape(group_rows)
    seq_first = jnp.max(
        jnp.where(seq_starts[None, :] <= places[:, None], seq_starts[None, :], 0), axis=1
    )
    cos_table, sine_table = rotary_tables(places - seq_first)
    gains = (norm1_gain[None, :], norm1_bias[None, :], norm2_gain[None, :], norm2_bias[None, :])
    first_all, second_all, hat, raw, grad_attended, grad_out = entry(
        spread, rows, gains, qkv_weight, out_weight
    )
    attended, grad_qkv, qkv_bias_part = attention(
        own.reshape(1),
        seq_starts,
        raw,
        qkv_bias[None, :],
        cos_table,
        sine_table,
        grad_attended,
        rows,
        names,
    )
    qkv_part = weight_product([first_all], [grad_qkv], True, bf16)
    out_part = weight_product([attended], [grad_out], False, bf16)
    qkv_sum, out_sum = lax.psum((qkv_part, out_part), "dp")

    plain = {n: (0, i * rows) for i, n in enumerate(names)}
    far = {n: (1, i * rows) for i, n in enumerate(names)}
    whole = Spread([second_all, grad_out], plain, far, names)
    hidden, grad_gate, gate_sum = mlp(whole, rows, up_weight, up_row, down_weight, False)
    branch = branch_sum(attended, hidden, out_weight, down_weight)
    scaled = input_sums(
        grad_qkv, grad_gate, qkv_weight, up_weight, gains[0], gains[2], hat
    )
    own_branch = scatter_group(*branch, names, mp, rows, True)
    own_scaled = scatter_group(*scaled[:2], names, mp, rows, False)
    layer_output = (input_float + own_branch + out_bias + down_bias).astype(bf16)
    input_grad = cotangent.astype(f32) + inv_std * (
        own_scaled
        - jnp.mean(own_scaled, axis=-1, keepdims=True)
        - xhat * jnp.mean(own_scaled * xhat, axis=-1, keepdims=True)
    )
    cot_sum = jnp.sum(cotangent.astype(f32), axis=0)
    small = jnp.concatenate([scaled[2].reshape(-1), cot_sum, qkv_bias_part.reshape(-1)])
    small = small.reshape(-1, 128)
    bit = 1
    while bit < dp:
        small = small + swap(small, "dp", dp, bit)
        bit *= 2
    small = small.reshape(-1)
    qkv_bias_grad = small[5 * width :]
    small = small[: 5 * width].reshape(-1, 128)
    bit = 1
    while bit < mp:
        small = small + swap(small, "mp", mp, bit)
        bit *= 2
    small = small.reshape(5, width)

    xhats, cots, hiddens, grads, sums = [second_all], [grad_out], [hidden], [grad_gate], [gate_sum]
    tie = corner if four else ()
    for pair in ring:
        if four:
            pair = after(pair, *tie)
            sides = spread_sides(pair, mp)
            tie = corner = spread_corner(*sides, mp)
            spread = spread_four(pair, sides, corner, mp)
        else:
            spread = spread_any(pair, mp)
        hidden, grad_gate, gate_sum, other_rows, other_cot = mlp(
            spread, rows, up_weight, up_row, down_weight, True
        )
        xhats.append(other_rows)
        cots.append(other_cot)
        hiddens.append(hidden)
        grads.append(grad_gate)
        sums.append(gate_sum)
    up_weight_grad = weight_product(xhats, grads, True, f32)
    down_weight_grad = weight_product(hiddens, cots, False, f32)
    up_bias_grad = sum(sums)[0]
    if lean:
        up_weight_grad, down_weight_grad, up_bias_grad = lax.psum(
            (up_weight_grad, down_weight_grad, up_bias_grad), "dp"
        )
    return (
        layer_output,
        input_grad,
        small[0],
        small[1],
        small[2],
        small[3],
        qkv_sum.astype(f32),
        qkv_bias_grad,
        out_sum.astype(f32),
        small[4],
        up_weight_grad,
        up_bias_grad,
        down_weight_grad,
        small[4],
    )


def solution(mesh):
    in_specs = (
        P(("dp", "mp"), None),
        P("dp", None),
        P(),
        P(),
        P(),
        P(),
        P(None, "mp"),
        P("mp"),
        P("mp", None),
        P(),
        P(None, "mp"),
        P("mp"),
        P("mp", None),
        P(),
        P(("dp", "mp"), None),
    )
    out_specs = (
        P(("dp", "mp"), None),
        P(("dp", "mp"), None),
        P(),
        P(),
        P(),
        P(),
        P(None, "mp"),
        P("mp"),
        P("mp", None),
        P(),
        P(None, "mp"),
        P("mp"),
        P("mp", None),
        P(),
    )
    return jax.shard_map(
        per_device, mesh=mesh, in_specs=in_specs, out_specs=out_specs, check_vma=False
    )
```

time: 1230 us -> 529 us (0.43)
  waiting for transfers between devices: 1000 us -> 261 us
  Pallas kernels: 0 us -> 182 us
  matrix products: 93.6 us -> 0 us
  blocking collectives: 42.9 us -> 0 us
  starting transfers between devices: 10.4 us -> 34.5 us
  local copies, waits for them, and re-layouts: 33.7 us -> 12.3 us
    psum x1, waiting for transfers between devices: 832 us -> 43.2 us  [per_device(): qkv_sum, out_sum = lax.psum((qkv_part, out_part), 'dp')]
    ppermute x0 -> x50, waiting for transfers between devices: none -> 217 us  [the longest x47 152 us: swap(): return lax.ppermute(value, axis, [(i, i ^ bit) for i in range(count)])]
    pallas_call x0 -> x12, Pallas kernels: none -> 182 us  [the longest x4 69.2 us: mlp(): call(functools.partial(mlp_body, spread=spread, rows=rows, block=block, t...]
    reduce_scatter x3 -> x0, waiting for transfers between devices: 99.3 us -> none  [the longest x1 69.6 us: per_device(): lax.psum_scatter(first_grad, 'mp', scatter_dimension=0, tiled=True)]
    dot_general x36 -> x0, matrix products: 93.6 us -> none  [the longest x12 29.8 us: contract_cols(): lax.dot_general(left, right, (((1,), (1,)), ((), ())), preferred_element_...]
    all_gather x3 -> x0, waiting for transfers between devices: 66.7 us -> none  [the longest x1 35.1 us: per_device(): lax.all_gather(second_own, 'mp', axis=0, tiled=True)]
    psum x2 -> x0, blocking collectives: 42.9 us -> none  [the longest x1 22.9 us: per_device(): lax.psum((gain_one, shift_one, gain_two, shift_two), 'mp')]
    ppermute x0 -> x50, starting transfers between devices: none -> 34.5 us  [the longest x47 31.1 us: swap(): return lax.ppermute(value, axis, [(i, i ^ bit) for i in range(count)])]
  transfers between devices with their start and end apart: 7 -> 51, of which waited for: 6 -> 20; matrix products, arithmetic and copies ran while one was open for 10% -> 4% of each run, Pallas kernels for 0% -> 11%
where the time goes in v1:
time: 529 us; the launch traced here: 525 us
  waiting for transfers between devices  261 us (49%)
  Pallas kernels  182 us (34%)
  starting transfers between devices  34.5 us (7%)
  other arithmetic  20.5 us (4%)
  between operations  15 us (3%)
  local copies, waits for them, and re-layouts  12.3 us (2%)
    ppermute x47, waiting for transfers between devices, swap(): return lax.ppermute(value, axis, [(i, i ^ bit) for i in range(count)])  152 us
    pallas_call x4, Pallas kernels, mlp(): call(functools.partial(mlp_body, spread=spread, rows=rows, block=block, t...  69.2 us
    ppermute x3, waiting for transfers between devices, turn(): lax.ppermute(value, axis, [(i, (i + step) % count) for i in range(count)])  65.3 us
    pallas_call x4, Pallas kernels, weight_product(): call(functools.partial(weight_body, pieces=len(lefts)), 'weight_product',...  61.5 us
    psum x1, waiting for transfers between devices, per_device(): qkv_sum, out_sum = lax.psum((qkv_part, out_part), 'dp')  43.2 us
    ppermute x47, starting transfers between devices, swap(): return lax.ppermute(value, axis, [(i, i ^ bit) for i in range(count)])  31.1 us
    pallas_call x1, Pallas kernels, input_sums(): call(input_body, 'input_sums', 2 * group_rows * width * depth, 2 * (group...  14.5 us
    pallas_call x1, Pallas kernels, entry(): call(functools.partial(entry_body, spread=spread, rows=rows, block=block)...  13.8 us
  transfers between devices with their start and end apart: 51, of which 20 were waited for; matrix products, arithmetic and copies ran while one was open for 4% of the time, Pallas kernels for 11%

profile of v1, /device:TPU:0, one launch (start us, length us, event | category | flops | bytes accessed | tf_op | source)
XLA Modules:
  0.0 525.0 jit_solution(10941981337805812097)
XLA Ops:
  7.3 1.1 constant_dynamic-update-slice_fusion.1
  8.3 1.1 constant_dynamic-update-slice_fusion.refs_0_
  9.4 3.0 collective-permute-start
  12.5 1.5 collective-permute-start.1
  14.3 21.4 %collective-permute-done.refs_1_ = bf16[256,2048]{1,0:T(8,128)(2,1)S(1)} collective-permute-done((bf16[256,2048]{1,0:T(8,128)(2,1)S(1)}, bf16[256,2048]{1,0:T(8,128)(2,1)S(1)}, u32[]{:S(2)}, u32[]{:S(2)}) %collective-permute-start) | collective-permute-done | bytes 1048608 | tf_op jit(solution)/shard_map/ppermute | solution.py:36
  35.7 1.8 collective-permute-start.2
  37.6 1.6 collective-permute-start.3
  40.4 8.5 %collective-permute-done.2.refs_3_ = bf16[128,2048]{1,0:T(8,128)(2,1)S(1)} collective-permute-done((bf16[128,2048]{1,0:T(8,128)(2,1)S(1)}, bf16[128,2048]{1,0:T(8,128)(2,1)S(1)}, u32[]{:S(2)}, u32[]{:S(2)}) %collective-permute-start.2) | collective-permute-done | bytes 524320 | tf_op jit(solution)/shard_map/ppermute | solution.py:36
  48.8 1.3 collective-permute-done.3.refs_4_
  50.9 1.9 fusion.15
  52.8 1.3 maximum_maximum_fusion
  54.3 1.0 copy-done.26
  55.3 1.0 copy-done.27
  56.3 13.8 %entry.1 = (bf16[1024,2048]{1,0:T(8,128)(2,1)}, bf16[1024,2048]{1,0:T(8,128)(2,1)}, bf16[1024,2048]{1,0:T(8,128)(2,1)}, f32[1024,768]{1,0:T(8,128)}, bf16[1024,2...) custom-call(bf16[256,2048]{1,0:T(8,128)(2,1)} %copy-done.10, bf16[256,2048]{1,0:T(8,128)(2,1)} %copy-done.8, ...), custom_call_target="tpu_custom_call" | custom-call | flops 4294967296 | bytes 25165824 | tf_op jit(solution)/shard_map/entry/pallas_call | solution.py:205
  70.1 15.8 %mlp.4 = (bf16[1024,1024]{1,0:T(8,128)(2,1)}, bf16[1024,1024]{1,0:T(8,128)(2,1)}, f32[1,1024]{1,0:T(1,128)}) custom-call(bf16[1024,2048]{1,0:T(8,128)(2,1)} %get-tuple-element.53.refs_0_, bf16[1024,2048]{1,0:T(8,128)(2,1)} %get-tuple-element.54.refs_1_.refs_4_, bf16[2048,1024]{1,0:T(8,128)(2,1)} %refs_10_.5, f32[1,1024]{1,0:T(1,128)} %bitcast.53, ...), custom_call_target="tpu_custom_call" | custom-call | flops 8589934592 | bytes 25165824 | tf_op jit(solution)/shard_map/mlp/pallas_call | solution.py:333
  85.9 13.4 %attention.1 = (bf16[1024,256]{1,0:T(8,128)(2,1)}, bf16[1024,768]{1,0:T(8,128)(2,1)}, f32[1,768]{1,0:T(1,128)}) custom-call(s32[1]{0:T(128)} %bitcast.own_ref, s32[4]{0:T(128)} %bitcast_subtract_fusion.1.starts_ref, f32[1024,768]{1,0:T(8,128)} %get-tuple-element.50.raw_ref, f32[1,768]{1,0:T(1,128)} %broadcast_in_dim.52.bias_ref, ...), custom_call_target="tpu_custom_call" | custom-call | flops 1610612736 | bytes 9437184 | tf_op jit(solution)/shard_map/attention/pallas_call | solution.py:576
  99.3 14.5 %input_sums.1 = (bf16[512,2048]{1,0:T(8,128)(2,1)}, bf16[512,2048]{1,0:T(8,128)(2,1)}, f32[4,2048]{1,0:T(4,128)}) custom-call(bf16[1024,768]{1,0:T(8,128)(2,1)} %get-tuple-element.58.qkv_grad_ref.refs_1_, bf16[1024,1024]{1,0:T(8,128)(2,1)} %get-tuple-element.59.gate_grad_ref.refs_4_, bf16[2048,768]{1,0:T(8,128)(2,1)} %qkv_ref.1, ...), custom_call_target="tpu_custom_call" | custom-call | flops 7516192768 | bytes 19398656 | tf_op jit(solution)/shard_map/input_sums/pallas_call | solution.py:449
  114.4 9.5 %branch_sum.1 = (bf16[512,2048]{1,0:T(8,128)(2,1)}, bf16[512,2048]{1,0:T(8,128)(2,1)}) custom-call(bf16[1024,256]{1,0:T(8,128)(2,1)} %get-tuple-element.52.attended_ref.refs_0_, bf16[1024,1024]{1,0:T(8,128)(2,1)} %get-tuple-element.55.hidden_ref.refs_0_, bf16[256,2048]{1,0:T(8,128)(2,1)} %out_ref.1, bf16[1024,2048]{1,0:T(8,128)(2,1)} %refs_12_.5), custom_call_target="tpu_custom_call" | custom-call | flops 5368709120 | bytes 12058624 | tf_op jit(solution)/shard_map/branch_sum/pallas_call | solution.py:408
  124.1 1.7 add_convert_fusion.4
  125.9 1.1 collective-permute-start.13
  127.0 1.2 collective-permute-done.9
  128.7 1.6 collective-permute-start.10
  130.6 20.9 %collective-permute-done.13 = bf16[256,2048]{1,0:T(8,128)(2,1)S(1)} collective-permute-done((bf16[256,2048]{1,0:T(8,128)(2,1)S(1)}, bf16[256,2048]{1,0:T(8,128)(2,1)S(1)}, u32[]{:S(2)}, u32[]{:S(2)}) %collective-permute-start.13) | collective-permute-done | bytes 1048608 | tf_op jit(solution)/shard_map/ppermute | solution.py:36
  151.5 1.3 add_convert_fusion
  152.8 1.6 collective-permute-start.14
  155.5 10.9 %collective-permute-done.14 = bf16[128,2048]{1,0:T(8,128)(2,1)S(1)} collective-permute-done((bf16[128,2048]{1,0:T(8,128)(2,1)S(1)}, bf16[128,2048]{1,0:T(8,128)(2,1)S(1)}, u32[]{:S(2)}, u32[]{:S(2)}) %collective-permute-start.14) | collective-permute-done | bytes 524320 | tf_op jit(solution)/shard_map/ppermute | solution.py:36
  166.3 1.6 fusion.14
  168.0 2.3 fusion.9
  170.4 1.6 collective-permute-start.20
  172.0 24.2 %collective-permute-done.20.refs_0_ = bf16[256,2048]{1,0:T(8,128)(2,1)} collective-permute-done((bf16[256,2048]{1,0:T(8,128)(2,1)S(1)}, bf16[256,2048]{1,0:T(8,128)(2,1)}, u32[]{:S(2)}, u32[]{:S(2)}) %collective-permute-start.20) | collective-permute-done | bytes 1048608 | tf_op jit(solution)/shard_map/ppermute | solution.py:40
  196.2 1.5 collective-permute-start.21
  197.9 7.3 %weight_product.4 = bf16[2048,768]{1,0:T(8,128)(2,1)} custom-call(bf16[1024,2048]{1,0:T(8,128)(2,1)} %get-tuple-element.65.refs_0_, bf16[1024,768]{1,0:T(8,128)(2,1)} %get-tuple-element.58.qkv_grad_ref.refs_1_), custom_call_target="tpu_custom_call" | custom-call | flops 3221225472 | bytes 12058624 | tf_op jit(solution)/shard_map/weight_product/pallas_call | solution.py:378
  205.2 1.7 collective-permute-start.30
  207.0 5.0 weight_product.5
  212.0 7.4 %collective-permute-done.21.refs_1_ = bf16[256,2048]{1,0:T(8,128)(2,1)S(1)} collective-permute-done((bf16[256,2048]{1,0:T(8,128)(2,1)}, bf16[256,2048]{1,0:T(8,128)(2,1)S(1)}, u32[]{:S(2)}, u32[]{:S(2)}) %collective-permute-start.21) | collective-permute-done | bytes 1048608 | tf_op jit(solution)/shard_map/ppermute | solution.py:36
  219.5 1.2 collective-permute-start.23
  220.7 1.4 collective-permute-done.22.refs_2_
  222.0 1.1 slice.173
  223.3 41.0 %collective-permute-done.30.refs_0_ = bf16[256,2048]{1,0:T(8,128)(2,1)} collective-permute-done((bf16[256,2048]{1,0:T(8,128)(2,1)S(1)}, bf16[256,2048]{1,0:T(8,128)(2,1)}, u32[]{:S(2)}, u32[]{:S(2)}) %collective-permute-start.30) | collective-permute-done | bytes 1048608 | tf_op jit(solution)/shard_map/ppermute | solution.py:40
  264.4 1.2 collective-permute-start.31
  265.6 1.6 collective-permute-start.32
  267.1 3.5 collective-permute-done.15
  270.7 36.1 %collective-permute-done.16 = f32[86,128]{1,0:T(8,128)S(1)} collective-permute-done((f32[86,128]{1,0:T(8,128)S(1)}, f32[86,128]{1,0:T(8,128)S(1)}, u32[]{:S(2)}, u32[]{:S(2)}) %collective-permute-start.16) | collective-permute-done | bytes 44064 | tf_op jit(solution)/shard_map/ppermute | solution.py:36
  308.4 1.9 collective-permute-start.18
  310.5 1.1 slice.175
  311.6 0.9 collective-permute-done.18
  312.4 1.8 collective-permute-start.34
  314.3 10.1 %collective-permute-done.33.refs_3_ = bf16[128,2048]{1,0:T(8,128)(2,1)} collective-permute-done((bf16[128,2048]{1,0:T(8,128)(2,1)S(1)}, bf16[128,2048]{1,0:T(8,128)(2,1)}, u32[]{:S(2)}, u32[]{:S(2)}) %collective-permute-start.33) | collective-permute-done | bytes 524320 | tf_op jit(solution)/shard_map/ppermute | solution.py:36
  324.6 1.4 collective-permute-done.34.refs_4_
  326.0 2.3 collective-permute-done.19
  330.6 23.6 %collective-permute-done.41.refs_1_ = bf16[256,2048]{1,0:T(8,128)(2,1)} collective-permute-done((bf16[256,2048]{1,0:T(8,128)(2,1)}, bf16[256,2048]{1,0:T(8,128)(2,1)}, u32[]{:S(2)}, u32[]{:S(2)}) %collective-permute-start.41) | collective-permute-done | bytes 1048608 | tf_op jit(solution)/shard_map/ppermute | solution.py:36
  356.0 43.2 %all-reduce.3.cloned.1.call-done = (bf16[2048,768]{1,0:T(8,128)(2,1)}, bf16[256,2048]{1,0:T(8,128)(2,1)}) async-done(((bf16[2048,768]{1,0:T(8,128)(2,1)}, bf16[256,2048]{1,0:T(8,128)(2,1)}), (bf16[2048,768]{1,0:T(8,128)(2,1)}, bf16[256,2048]{1,0:T(8,128)(2,1)})) %all-reduce.3.cloned.1.call-update) | async-done | bytes 4194320 | tf_op jit(solution)/shard_map/psum | solution.py:708
  399.2 5.2 convert_element_type.190
  404.4 1.6 convert_element_type.191
  406.0 1.1 slice.176
  407.2 1.5 collective-permute-start.43
  408.8 1.5 collective-permute-start.44
  410.8 18.1 %mlp.5 = (bf16[1024,1024]{1,0:T(8,128)(2,1)}, bf16[1024,1024]{1,0:T(8,128)(2,1)}, f32[1,1024]{1,0:T(1,128)}, bf16[1024,2048]{1,0:T(8,128)(2,1)}, bf16[1024,2048]{1,0:T(8,128)(2,1)}) custom-call(bf16[256,2048]{1,0:T(8,128)(2,1)} %collective-permute-done.20.refs_0_, bf16[256,2048]{1,0:T(8,128)(2,1)} %copy-done.5, ...), custom_call_target="tpu_custom_call" | custom-call | flops 8589934592 | bytes 25165824 | tf_op jit(solution)/shard_map/mlp/pallas_call | solution.py:333
  429.5 17.6 %mlp.6 = (bf16[1024,1024]{1,0:T(8,128)(2,1)}, bf16[1024,1024]{1,0:T(8,128)(2,1)}, f32[1,1024]{1,0:T(1,128)}, bf16[1024,2048]{1,0:T(8,128)(2,1)}, bf16[1024,2048]{1,0:T(8,128)(2,1)}) custom-call(bf16[256,2048]{1,0:T(8,128)(2,1)} %collective-permute-done.30.refs_0_, bf16[256,2048]{1,0:T(8,128)(2,1)} %copy-done.6, ...), custom_call_target="tpu_custom_call" | custom-call | flops 8589934592 | bytes 25165824 | tf_op jit(solution)/shard_map/mlp/pallas_call | solution.py:333
  447.2 0.9 copy-done.25
  449.2 17.7 %mlp.7 = (bf16[1024,1024]{1,0:T(8,128)(2,1)}, bf16[1024,1024]{1,0:T(8,128)(2,1)}, f32[1,1024]{1,0:T(1,128)}, bf16[1024,2048]{1,0:T(8,128)(2,1)}, bf16[1024,2048]{1,0:T(8,128)(2,1)}) custom-call(bf16[256,2048]{1,0:T(8,128)(2,1)} %collective-permute-done.40.refs_0_, bf16[256,2048]{1,0:T(8,128)(2,1)} %collective-permute-done.41.refs_1_, ...), custom_call_target="tpu_custom_call" | custom-call | flops 8589934592 | bytes 25165824 | tf_op jit(solution)/shard_map/mlp/pallas_call | solution.py:333
  466.9 1.3 add_add_fusion
  468.2 24.7 %weight_product.7 = f32[1024,2048]{1,0:T(8,128)} custom-call(bf16[1024,1024]{1,0:T(8,128)(2,1)} %get-tuple-element.55.hidden_ref.refs_0_, bf16[1024,1024]{1,0:T(8,128)(2,1)} %get-tuple-element.80.refs_1_, bf16[1024,1024]{1,0:T(8,128)(2,1)} %get-tuple-element.81.refs_2_, bf16[1024,1024]{1,0:T(8,128)(2,1)} %get-tuple-element.82.refs_3_, ...), custom_call_target="tpu_custom_call" | custom-call | flops 17179869184 | bytes 33554432 | tf_op jit(solution)/shard_map/weight_product/pallas_call | solution.py:378
  492.9 24.5 %weight_product.6 = f32[2048,1024]{1,0:T(8,128)} custom-call(bf16[1024,2048]{1,0:T(8,128)(2,1)} %get-tuple-element.53.refs_0_, bf16[1024,2048]{1,0:T(8,128)(2,1)} %get-tuple-element.67.refs_1_, bf16[1024,2048]{1,0:T(8,128)(2,1)} %get-tuple-element.69.refs_2_, bf16[1024,2048]{1,0:T(8,128)(2,1)} %get-tuple-element.72.refs_3_, ...), custom_call_target="tpu_custom_call" | custom-call | flops 17179869184 | bytes 33554432 | tf_op jit(solution)/shard_map/weight_product/pallas_call | solution.py:378
  (184 shorter events, 14.6 us)
Async XLA Ops:
  7.2 43.1 %copy-start.20 = (f32[768]{0:T(1024)S(1)}, f32[768]{0:T(1024)}, u32[]{:S(2)}) copy-start(f32[768]{0:T(1024)} %param.23) | copy-start | bytes 9220
  7.2 392.0 %all-reduce.3.cloned.1.call-start = ((), (), s32[]{:S(2)}) async-start(), calls=%async_computation | async-start | bytes 8388608 | tf_op jit(solution)/shard_map/psum | solution.py:708
  9.4 44.8 %copy-start.10 = (bf16[256,2048]{1,0:T(8,128)(2,1)}, bf16[256,2048]{1,0:T(8,128)(2,1)S(1)}, u32[]{:S(2)}) copy-start(bf16[256,2048]{1,0:T(8,128)(2,1)S(1)} %constant_dynamic-update-slice_fusion.refs_0_) | copy-start | bytes 3145732
  9.4 26.2 %collective-permute-start = (bf16[256,2048]{1,0:T(8,128)(2,1)S(1)}, bf16[256,2048]{1,0:T(8,128)(2,1)S(1)}, u32[]{:S(2)}, u32[]{:S(2)}) collective-permute-start(bf16[256,2048]{1,0:T(8,128)(2,1)S(1)} %constant_dynamic-update-slice_fusion.refs_0_), channel_id=1, source_target_pairs={{0,2},{1,3},{2,0},{3,1},{4,6},{5,7},{6,4},{7,5},{8,10},{9,11},{10,... | collective-permute-start | bytes 3145736 | tf_op jit(solution)/shard_map/ppermute | solution.py:36
  12.5 25.0 %collective-permute-start.1 = (bf16[256,2048]{1,0:T(8,128)(2,1)S(1)}, bf16[256,2048]{1,0:T(8,128)(2,1)S(1)}, u32[]{:S(2)}, u32[]{:S(2)}) collective-permute-start(bf16[256,2048]{1,0:T(8,128)(2,1)S(1)} %constant_dynamic-update-slice_fusion.refs_0_), channel_id=1, source_target_pairs={{0,4},{1,5},{2,6},{3,7},{4,0},{5,1},{6,2},{7,3},{8,12},{9,13},{10,... | collective-permute-start | bytes 3145736 | tf_op jit(solution)/shard_map/ppermute | solution.py:36
  14.0 40.2 %collective-permute-start.4 = (bf16[256,2048]{1,0:T(8,128)(2,1)S(1)}, bf16[256,2048]{1,0:T(8,128)(2,1)}, u32[]{:S(2)}, u32[]{:S(2)}) collective-permute-start(bf16[256,2048]{1,0:T(8,128)(2,1)S(1)} %constant_dynamic-update-slice_fusion.refs_0_), channel_id=1, source_target_pairs={{0,1},{1,0},{2,3},{3,2},{4,5},{5,4},{6,7},{7,6},{8,9},{9,8},{10,11... | collective-permute-start | bytes 3145736 | tf_op jit(solution)/shard_map/ppermute | solution.py:36
  35.7 13.2 %collective-permute-start.2 = (bf16[128,2048]{1,0:T(8,128)(2,1)S(1)}, bf16[128,2048]{1,0:T(8,128)(2,1)S(1)}, u32[]{:S(2)}, u32[]{:S(2)}) collective-permute-start(bf16[128,2048]{1,0:T(8,128)(2,1)S(1)} %slice.151), channel_id=1, source_target_pairs={{0,4},{1,5},{2,6},{3,7},{4,0},{5,1},{6,2},{7,3},{8,12},{9,13},{10,... | collective-permute-start | bytes 1572872 | tf_op jit(solution)/shard_map/ppermute | solution.py:36
  37.6 12.6 %collective-permute-start.3 = (bf16[128,2048]{1,0:T(8,128)(2,1)S(1)}, bf16[128,2048]{1,0:T(8,128)(2,1)S(1)}, u32[]{:S(2)}, u32[]{:S(2)}) collective-permute-start(bf16[128,2048]{1,0:T(8,128)(2,1)S(1)} %slice.152), channel_id=1, source_target_pairs={{0,2},{1,3},{2,0},{3,1},{4,6},{5,7},{6,4},{7,5},{8,10},{9,11},{10,... | collective-permute-start | bytes 1572872 | tf_op jit(solution)/shard_map/ppermute | solution.py:36
  39.2 15.1 %collective-permute-start.5 = (bf16[256,2048]{1,0:T(8,128)(2,1)S(1)}, bf16[256,2048]{1,0:T(8,128)(2,1)S(1)}, u32[]{:S(2)}, u32[]{:S(2)}) collective-permute-start(bf16[256,2048]{1,0:T(8,128)(2,1)S(1)} %collective-permute-done.refs_1_), channel_id=1, source_target_pairs={{0,1},{1,0},{2,3},{3,2},{4,5},{5,4},{6,7},{7,6},{8,9},{9,8},{10,11... | collective-permute-start | bytes 3145736 | tf_op jit(solution)/shard_map/ppermute | solution.py:36
  39.3 15.0 %collective-permute-start.6 = (bf16[256,2048]{1,0:T(8,128)(2,1)S(1)}, bf16[256,2048]{1,0:T(8,128)(2,1)S(1)}, u32[]{:S(2)}, u32[]{:S(2)}) collective-permute-start(bf16[256,2048]{1,0:T(8,128)(2,1)S(1)} %collective-permute-done.1.refs_2_), channel_id=1, source_target_pairs={{0,1},{1,0},{2,3},{3,2},{4,5},{5,4},{6,7},{7,6},{8,9},{9,8},{10,11... | collective-permute-start | bytes 3145736 | tf_op jit(solution)/shard_map/ppermute | solution.py:36
  48.8 5.4 %collective-permute-start.7 = (bf16[128,2048]{1,0:T(8,128)(2,1)S(1)}, bf16[128,2048]{1,0:T(8,128)(2,1)S(1)}, u32[]{:S(2)}, u32[]{:S(2)}) collective-permute-start(bf16[128,2048]{1,0:T(8,128)(2,1)S(1)} %collective-permute-done.2.refs_3_), channel_id=1, source_target_pairs={{0,1},{1,0},{2,3},{3,2},{4,5},{5,4},{6,7},{7,6},{8,9},{9,8},{10,11... | collective-permute-start | bytes 1572872 | tf_op jit(solution)/shard_map/ppermute | solution.py:36
  50.2 4.1 collective-permute-start.8
  113.8 10.3 %collective-permute-start.12 = (bf16[512,2048]{1,0:T(8,128)(2,1)}, bf16[512,2048]{1,0:T(8,128)(2,1)}, u32[]{:S(2)}, u32[]{:S(2)}) collective-permute-start(bf16[512,2048]{1,0:T(8,128)(2,1)} %get-tuple-element.62), channel_id=1, source_target_pairs={{0,1},{1,0},{2,3},{3,2},{4,5},{5,4},{6,7},{7,6},{8,9},{9,8},{10,11... | collective-permute-start | bytes 6291464 | tf_op jit(solution)/shard_map/ppermute | solution.py:36
  123.9 4.4 collective-permute-start.9
  125.9 25.6 %collective-permute-start.13 = (bf16[256,2048]{1,0:T(8,128)(2,1)S(1)}, bf16[256,2048]{1,0:T(8,128)(2,1)S(1)}, u32[]{:S(2)}, u32[]{:S(2)}) collective-permute-start(bf16[256,2048]{1,0:T(8,128)(2,1)S(1)} %pad_maximum_fusion.1), channel_id=1, source_target_pairs={{0,4},{1,5},{2,6},{3,7},{4,0},{5,1},{6,2},{7,3},{8,12},{9,13},{10,... | collective-permute-start | bytes 3145736 | tf_op jit(solution)/shard_map/ppermute | solution.py:36
  128.7 25.6 %collective-permute-start.10 = (bf16[256,2048]{1,0:T(8,128)(2,1)S(1)}, bf16[256,2048]{1,0:T(8,128)(2,1)S(1)}, u32[]{:S(2)}, u32[]{:S(2)}) collective-permute-start(bf16[256,2048]{1,0:T(8,128)(2,1)S(1)} %pad_maximum_fusion), channel_id=1, source_target_pairs={{0,2},{1,3},{2,0},{3,1},{4,6},{5,7},{6,4},{7,5},{8,10},{9,11},{10,... | collective-permute-start | bytes 3145736 | tf_op jit(solution)/shard_map/ppermute | solution.py:36
  152.8 13.5 %collective-permute-start.14 = (bf16[128,2048]{1,0:T(8,128)(2,1)S(1)}, bf16[128,2048]{1,0:T(8,128)(2,1)S(1)}, u32[]{:S(2)}, u32[]{:S(2)}) collective-permute-start(bf16[128,2048]{1,0:T(8,128)(2,1)S(1)} %add_convert_fusion), channel_id=1, source_target_pairs={{0,2},{1,3},{2,0},{3,1},{4,6},{5,7},{6,4},{7,5},{8,10},{9,11},{10,... | collective-permute-start | bytes 1572872 | tf_op jit(solution)/shard_map/ppermute | solution.py:36
  154.7 13.2 %collective-permute-start.11 = (bf16[128,2048]{1,0:T(8,128)(2,1)S(1)}, bf16[128,2048]{1,0:T(8,128)(2,1)S(1)}, u32[]{:S(2)}, u32[]{:S(2)}) collective-permute-start(bf16[128,2048]{1,0:T(8,128)(2,1)S(1)} %add_convert_fusion.6), channel_id=1, source_target_pairs={{0,4},{1,5},{2,6},{3,7},{4,0},{5,1},{6,2},{7,3},{8,12},{9,13},{10,... | collective-permute-start | bytes 1572872 | tf_op jit(solution)/shard_map/ppermute | solution.py:36
  170.4 25.8 %collective-permute-start.20 = (bf16[256,2048]{1,0:T(8,128)(2,1)S(1)}, bf16[256,2048]{1,0:T(8,128)(2,1)}, u32[]{:S(2)}, u32[]{:S(2)}) collective-permute-start(bf16[256,2048]{1,0:T(8,128)(2,1)S(1)} %pad_maximum_fusion.2), channel_id=1, source_target_pairs={{0,8},{8,16},{16,24},{24,0},{1,9},{9,17},{17,25},{25,1},{2,10},{10... | collective-permute-start | bytes 3145736 | tf_op jit(solution)/shard_map/ppermute | solution.py:40
  196.2 23.2 %collective-permute-start.21 = (bf16[256,2048]{1,0:T(8,128)(2,1)}, bf16[256,2048]{1,0:T(8,128)(2,1)S(1)}, u32[]{:S(2)}, u32[]{:S(2)}) collective-permute-start(bf16[256,2048]{1,0:T(8,128)(2,1)} %collective-permute-done.20.refs_0_), channel_id=1, source_target_pairs={{0,2},{1,3},{2,0},{3,1},{4,6},{5,7},{6,4},{7,5},{8,10},{9,11},{10,... | collective-permute-start | bytes 3145736 | tf_op jit(solution)/shard_map/ppermute | solution.py:36
  197.7 24.3 %collective-permute-start.22 = (bf16[256,2048]{1,0:T(8,128)(2,1)}, bf16[256,2048]{1,0:T(8,128)(2,1)}, u32[]{:S(2)}, u32[]{:S(2)}) collective-permute-start(bf16[256,2048]{1,0:T(8,128)(2,1)} %collective-permute-done.20.refs_0_), channel_id=1, source_target_pairs={{0,4},{1,5},{2,6},{3,7},{4,0},{5,1},{6,2},{7,3},{8,12},{9,13},{10,... | collective-permute-start | bytes 3145736 | tf_op jit(solution)/shard_map/ppermute | solution.py:36
  205.2 59.2 %collective-permute-start.30 = (bf16[256,2048]{1,0:T(8,128)(2,1)S(1)}, bf16[256,2048]{1,0:T(8,128)(2,1)}, u32[]{:S(2)}, u32[]{:S(2)}) collective-permute-start(bf16[256,2048]{1,0:T(8,128)(2,1)S(1)} %pad_maximum_fusion.2), channel_id=1, source_target_pairs={{0,24},{8,0},{16,8},{24,16},{1,25},{9,1},{17,9},{25,17},{2,26},{10... | collective-permute-start | bytes 3145736 | tf_op jit(solution)/shard_map/ppermute | solution.py:40
  219.4 92.1 %copy-start.5 = (bf16[256,2048]{1,0:T(8,128)(2,1)}, bf16[256,2048]{1,0:T(8,128)(2,1)S(1)}, u32[]{:S(2)}) copy-start(bf16[256,2048]{1,0:T(8,128)(2,1)S(1)} %collective-permute-done.21.refs_1_) | copy-start | bytes 3145732
  219.5 44.9 %collective-permute-start.23 = (bf16[128,2048]{1,0:T(8,128)(2,1)S(1)}, bf16[128,2048]{1,0:T(8,128)(2,1)}, u32[]{:S(2)}, u32[]{:S(2)}) collective-permute-start(bf16[128,2048]{1,0:T(8,128)(2,1)S(1)} %slice.172), channel_id=1, source_target_pairs={{0,4},{1,5},{2,6},{3,7},{4,0},{5,1},{6,2},{7,3},{8,12},{9,13},{10,... | collective-permute-start | bytes 1572872 | tf_op jit(solution)/shard_map/ppermute | solution.py:36
  223.1 41.3 %collective-permute-start.24 = (bf16[128,2048]{1,0:T(8,128)(2,1)S(1)}, bf16[128,2048]{1,0:T(8,128)(2,1)}, u32[]{:S(2)}, u32[]{:S(2)}) collective-permute-start(bf16[128,2048]{1,0:T(8,128)(2,1)S(1)} %slice.173), channel_id=1, source_target_pairs={{0,2},{1,3},{2,0},{3,1},{4,6},{5,7},{6,4},{7,5},{8,10},{9,11},{10,... | collective-permute-start | bytes 1572872 | tf_op jit(solution)/shard_map/ppermute | solution.py:36
  223.3 47.4 %collective-permute-start.15 = (f32[86,128]{1,0:T(8,128)S(1)}, f32[86,128]{1,0:T(8,128)S(1)}, u32[]{:S(2)}, u32[]{:S(2)}) collective-permute-start(f32[86,128]{1,0:T(8,128)S(1)} %maximum_bitcast_fusion), channel_id=1, source_target_pairs={{0,8},{8,0},{16,24},{24,16},{1,9},{9,1},{17,25},{25,17},{2,10},{10... | collective-permute-start | bytes 132104 | tf_op jit(solution)/shard_map/ppermute | solution.py:36
  264.4 44.0 %collective-permute-start.31 = (bf16[256,2048]{1,0:T(8,128)(2,1)}, bf16[256,2048]{1,0:T(8,128)(2,1)S(1)}, u32[]{:S(2)}, u32[]{:S(2)}) collective-permute-start(bf16[256,2048]{1,0:T(8,128)(2,1)} %collective-permute-done.30.refs_0_), channel_id=1, source_target_pairs={{0,2},{1,3},{2,0},{3,1},{4,6},{5,7},{6,4},{7,5},{8,10},{9,11},{10,... | collective-permute-start | bytes 3145736 | tf_op jit(solution)/shard_map/ppermute | solution.py:36
  265.6 44.7 %collective-permute-start.32 = (bf16[256,2048]{1,0:T(8,128)(2,1)}, bf16[256,2048]{1,0:T(8,128)(2,1)}, u32[]{:S(2)}, u32[]{:S(2)}) collective-permute-start(bf16[256,2048]{1,0:T(8,128)(2,1)} %collective-permute-done.30.refs_0_), channel_id=1, source_target_pairs={{0,4},{1,5},{2,6},{3,7},{4,0},{5,1},{6,2},{7,3},{8,12},{9,13},{10,... | collective-permute-start | bytes 3145736 | tf_op jit(solution)/shard_map/ppermute | solution.py:36
  267.1 47.1 %collective-permute-start.40 = (bf16[256,2048]{1,0:T(8,128)(2,1)}, bf16[256,2048]{1,0:T(8,128)(2,1)}, u32[]{:S(2)}, u32[]{:S(2)}) collective-permute-start(bf16[256,2048]{1,0:T(8,128)(2,1)} %collective-permute-done.20.refs_0_), channel_id=1, source_target_pairs={{0,8},{8,16},{16,24},{24,0},{1,9},{9,17},{17,25},{25,1},{2,10},{10... | collective-permute-start | bytes 3145736 | tf_op jit(solution)/shard_map/ppermute | solution.py:40
  270.7 36.2 %collective-permute-start.16 = (f32[86,128]{1,0:T(8,128)S(1)}, f32[86,128]{1,0:T(8,128)S(1)}, u32[]{:S(2)}, u32[]{:S(2)}) collective-permute-start(f32[86,128]{1,0:T(8,128)S(1)} %fusion.17), channel_id=1, source_target_pairs={{0,16},{8,24},{16,0},{24,8},{1,17},{9,25},{17,1},{25,9},{2,18},{10... | collective-permute-start | bytes 132104 | tf_op jit(solution)/shard_map/ppermute | solution.py:36
  306.9 1.3 collective-permute-start.17
  307.0 21.4 %collective-permute-start.25 = (bf16[256,2048]{1,0:T(8,128)(2,1)}, bf16[256,2048]{1,0:T(8,128)(2,1)S(1)}, u32[]{:S(2)}, u32[]{:S(2)}) collective-permute-start(bf16[256,2048]{1,0:T(8,128)(2,1)} %collective-permute-done.20.refs_0_), channel_id=1, source_target_pairs={{0,1},{1,0},{2,3},{3,2},{4,5},{5,4},{6,7},{7,6},{8,9},{9,8},{10,11... | collective-permute-start | bytes 3145736 | tf_op jit(solution)/shard_map/ppermute | solution.py:36
  308.2 20.5 %collective-permute-start.26 = (bf16[256,2048]{1,0:T(8,128)(2,1)S(1)}, bf16[256,2048]{1,0:T(8,128)(2,1)S(1)}, u32[]{:S(2)}, u32[]{:S(2)}) collective-permute-start(bf16[256,2048]{1,0:T(8,128)(2,1)S(1)} %collective-permute-done.21.refs_1_), channel_id=1, source_target_pairs={{0,1},{1,0},{2,3},{3,2},{4,5},{5,4},{6,7},{7,6},{8,9},{9,8},{10,11... | collective-permute-start | bytes 3145736 | tf_op jit(solution)/shard_map/ppermute | solution.py:36
  308.4 96.0 %copy-start.6 = (bf16[256,2048]{1,0:T(8,128)(2,1)}, bf16[256,2048]{1,0:T(8,128)(2,1)S(1)}, u32[]{:S(2)}) copy-start(bf16[256,2048]{1,0:T(8,128)(2,1)S(1)} %collective-permute-done.31.refs_1_) | copy-start | bytes 3145732
  308.4 4.1 collective-permute-start.18
  310.3 14.1 %collective-permute-start.33 = (bf16[128,2048]{1,0:T(8,128)(2,1)S(1)}, bf16[128,2048]{1,0:T(8,128)(2,1)}, u32[]{:S(2)}, u32[]{:S(2)}) collective-permute-start(bf16[128,2048]{1,0:T(8,128)(2,1)S(1)} %slice.174), channel_id=1, source_target_pairs={{0,4},{1,5},{2,6},{3,7},{4,0},{5,1},{6,2},{7,3},{8,12},{9,13},{10,... | collective-permute-start | bytes 1572872 | tf_op jit(solution)/shard_map/ppermute | solution.py:36
  312.4 13.6 %collective-permute-start.34 = (bf16[128,2048]{1,0:T(8,128)(2,1)S(1)}, bf16[128,2048]{1,0:T(8,128)(2,1)}, u32[]{:S(2)}, u32[]{:S(2)}) collective-permute-start(bf16[128,2048]{1,0:T(8,128)(2,1)S(1)} %slice.175), channel_id=1, source_target_pairs={{0,2},{1,3},{2,0},{3,1},{4,6},{5,7},{6,4},{7,5},{8,10},{9,11},{10,... | collective-permute-start | bytes 1572872 | tf_op jit(solution)/shard_map/ppermute | solution.py:36
  314.2 15.1 %collective-permute-start.27 = (bf16[256,2048]{1,0:T(8,128)(2,1)}, bf16[256,2048]{1,0:T(8,128)(2,1)S(1)}, u32[]{:S(2)}, u32[]{:S(2)}) collective-permute-start(bf16[256,2048]{1,0:T(8,128)(2,1)} %collective-permute-done.22.refs_2_), channel_id=1, source_target_pairs={{0,1},{1,0},{2,3},{3,2},{4,5},{5,4},{6,7},{7,6},{8,9},{9,8},{10,11... | collective-permute-start | bytes 3145736 | tf_op jit(solution)/shard_map/ppermute | solution.py:36
  324.4 4.0 collective-permute-start.19
  326.0 3.4 collective-permute-start.28
  328.4 2.1 collective-permute-start.29
  328.4 27.6 %copy-start.22 = (bf16[256,2048]{1,0:T(8,128)(2,1)}, bf16[256,2048]{1,0:T(8,128)(2,1)S(1)}, u32[]{:S(2)}) copy-start(bf16[256,2048]{1,0:T(8,128)(2,1)S(1)} %collective-permute-done.25.refs_5_) | copy-start | bytes 3145732
  328.4 25.9 %collective-permute-start.41 = (bf16[256,2048]{1,0:T(8,128)(2,1)}, bf16[256,2048]{1,0:T(8,128)(2,1)}, u32[]{:S(2)}, u32[]{:S(2)}) collective-permute-start(bf16[256,2048]{1,0:T(8,128)(2,1)} %collective-permute-done.40.refs_0_), channel_id=1, source_target_pairs={{0,2},{1,3},{2,0},{3,1},{4,6},{5,7},{6,4},{7,5},{8,10},{9,11},{10,... | collective-permute-start | bytes 3145736 | tf_op jit(solution)/shard_map/ppermute | solution.py:36
  328.7 27.3 %copy-start.23 = (bf16[256,2048]{1,0:T(8,128)(2,1)}, bf16[256,2048]{1,0:T(8,128)(2,1)S(1)}, u32[]{:S(2)}) copy-start(bf16[256,2048]{1,0:T(8,128)(2,1)S(1)} %collective-permute-done.26.refs_6_) | copy-start | bytes 3145732
  328.7 25.5 %collective-permute-start.42 = (bf16[256,2048]{1,0:T(8,128)(2,1)}, bf16[256,2048]{1,0:T(8,128)(2,1)S(1)}, u32[]{:S(2)}, u32[]{:S(2)}) collective-permute-start(bf16[256,2048]{1,0:T(8,128)(2,1)} %collective-permute-done.40.refs_0_), channel_id=1, source_target_pairs={{0,4},{1,5},{2,6},{3,7},{4,0},{5,1},{6,2},{7,3},{8,12},{9,13},{10,... | collective-permute-start | bytes 3145736 | tf_op jit(solution)/shard_map/ppermute | solution.py:36
  329.4 26.6 %copy-start.24 = (bf16[256,2048]{1,0:T(8,128)(2,1)}, bf16[256,2048]{1,0:T(8,128)(2,1)S(1)}, u32[]{:S(2)}) copy-start(bf16[256,2048]{1,0:T(8,128)(2,1)S(1)} %collective-permute-done.27.refs_7_) | copy-start | bytes 3145732
  329.4 77.7 %collective-permute-start.35 = (bf16[256,2048]{1,0:T(8,128)(2,1)}, bf16[256,2048]{1,0:T(8,128)(2,1)}, u32[]{:S(2)}, u32[]{:S(2)}) collective-permute-start(bf16[256,2048]{1,0:T(8,128)(2,1)} %collective-permute-done.30.refs_0_), channel_id=1, source_target_pairs={{0,1},{1,0},{2,3},{3,2},{4,5},{5,4},{6,7},{7,6},{8,9},{9,8},{10,11... | collective-permute-start | bytes 3145736 | tf_op jit(solution)/shard_map/ppermute | solution.py:36
  329.4 26.6 %copy-start.28 = (bf16[128,2048]{1,0:T(8,128)(2,1)}, bf16[128,2048]{1,0:T(8,128)(2,1)S(1)}, u32[]{:S(2)}) copy-start(bf16[128,2048]{1,0:T(8,128)(2,1)S(1)} %collective-permute-done.28.refs_8_) | copy-start | bytes 1572868
  329.4 77.8 %collective-permute-start.36 = (bf16[256,2048]{1,0:T(8,128)(2,1)S(1)}, bf16[256,2048]{1,0:T(8,128)(2,1)}, u32[]{:S(2)}, u32[]{:S(2)}) collective-permute-start(bf16[256,2048]{1,0:T(8,128)(2,1)S(1)} %collective-permute-done.31.refs_1_), channel_id=1, source_target_pairs={{0,1},{1,0},{2,3},{3,2},{4,5},{5,4},{6,7},{7,6},{8,9},{9,8},{10,11... | collective-permute-start | bytes 3145736 | tf_op jit(solution)/shard_map/ppermute | solution.py:36
  330.5 25.5 %copy-start.29 = (bf16[128,2048]{1,0:T(8,128)(2,1)}, bf16[128,2048]{1,0:T(8,128)(2,1)S(1)}, u32[]{:S(2)}) copy-start(bf16[128,2048]{1,0:T(8,128)(2,1)S(1)} %collective-permute-done.29.refs_9_) | copy-start | bytes 1572868
  330.5 78.3 %collective-permute-start.37 = (bf16[256,2048]{1,0:T(8,128)(2,1)}, bf16[256,2048]{1,0:T(8,128)(2,1)}, u32[]{:S(2)}, u32[]{:S(2)}) collective-permute-start(bf16[256,2048]{1,0:T(8,128)(2,1)} %collective-permute-done.32.refs_2_), channel_id=1, source_target_pairs={{0,1},{1,0},{2,3},{3,2},{4,5},{5,4},{6,7},{7,6},{8,9},{9,8},{10,11... | collective-permute-start | bytes 3145736 | tf_op jit(solution)/shard_map/ppermute | solution.py:36
  354.3 56.0 %collective-permute-start.38 = (bf16[128,2048]{1,0:T(8,128)(2,1)}, bf16[128,2048]{1,0:T(8,128)(2,1)S(1)}, u32[]{:S(2)}, u32[]{:S(2)}) collective-permute-start(bf16[128,2048]{1,0:T(8,128)(2,1)} %collective-permute-done.33.refs_3_), channel_id=1, source_target_pairs={{0,1},{1,0},{2,3},{3,2},{4,5},{5,4},{6,7},{7,6},{8,9},{9,8},{10,11... | collective-permute-start | bytes 1572872 | tf_op jit(solution)/shard_map/ppermute | solution.py:36
  354.3 56.0 %copy-start.7 = (bf16[256,2048]{1,0:T(8,128)(2,1)}, bf16[256,2048]{1,0:T(8,128)(2,1)S(1)}, u32[]{:S(2)}) copy-start(bf16[256,2048]{1,0:T(8,128)(2,1)S(1)} %collective-permute-done.42.refs_2_) | copy-start | bytes 3145732
  354.3 56.0 %collective-permute-start.39 = (bf16[128,2048]{1,0:T(8,128)(2,1)}, bf16[128,2048]{1,0:T(8,128)(2,1)}, u32[]{:S(2)}, u32[]{:S(2)}) collective-permute-start(bf16[128,2048]{1,0:T(8,128)(2,1)} %collective-permute-done.34.refs_4_), channel_id=1, source_target_pairs={{0,1},{1,0},{2,3},{3,2},{4,5},{5,4},{6,7},{7,6},{8,9},{9,8},{10,11... | collective-permute-start | bytes 1572872 | tf_op jit(solution)/shard_map/ppermute | solution.py:36
  356.0 161.4 %copy-start.11 = (f32[2048]{0:T(1024)}, f32[2048]{0:T(1024)S(1)}, u32[]{:S(2)}) copy-start(f32[2048]{0:T(1024)S(1)} %get-tuple-element.136) | copy-start | bytes 24580
  407.1 40.0 %collective-permute-start.45 = (bf16[256,2048]{1,0:T(8,128)(2,1)}, bf16[256,2048]{1,0:T(8,128)(2,1)}, u32[]{:S(2)}, u32[]{:S(2)}) collective-permute-start(bf16[256,2048]{1,0:T(8,128)(2,1)} %collective-permute-done.40.refs_0_), channel_id=1, source_target_pairs={{0,1},{1,0},{2,3},{3,2},{4,5},{5,4},{6,7},{7,6},{8,9},{9,8},{10,11... | collective-permute-start | bytes 3145736 | tf_op jit(solution)/shard_map/ppermute | solution.py:36
  407.2 21.7 %collective-permute-start.43 = (bf16[128,2048]{1,0:T(8,128)(2,1)S(1)}, bf16[128,2048]{1,0:T(8,128)(2,1)}, u32[]{:S(2)}, u32[]{:S(2)}) collective-permute-start(bf16[128,2048]{1,0:T(8,128)(2,1)S(1)} %slice.176), channel_id=1, source_target_pairs={{0,4},{1,5},{2,6},{3,7},{4,0},{5,1},{6,2},{7,3},{8,12},{9,13},{10,... | collective-permute-start | bytes 1572872 | tf_op jit(solution)/shard_map/ppermute | solution.py:36
  408.8 20.3 %collective-permute-start.44 = (bf16[128,2048]{1,0:T(8,128)(2,1)S(1)}, bf16[128,2048]{1,0:T(8,128)(2,1)}, u32[]{:S(2)}, u32[]{:S(2)}) collective-permute-start(bf16[128,2048]{1,0:T(8,128)(2,1)S(1)} %slice.177), channel_id=1, source_target_pairs={{0,2},{1,3},{2,0},{3,1},{4,6},{5,7},{6,4},{7,5},{8,10},{9,11},{10,... | collective-permute-start | bytes 1572872 | tf_op jit(solution)/shard_map/ppermute | solution.py:36
  410.2 36.9 %collective-permute-start.46 = (bf16[256,2048]{1,0:T(8,128)(2,1)}, bf16[256,2048]{1,0:T(8,128)(2,1)S(1)}, u32[]{:S(2)}, u32[]{:S(2)}) collective-permute-start(bf16[256,2048]{1,0:T(8,128)(2,1)} %collective-permute-done.41.refs_1_), channel_id=1, source_target_pairs={{0,1},{1,0},{2,3},{3,2},{4,5},{5,4},{6,7},{7,6},{8,9},{9,8},{10,11... | collective-permute-start | bytes 3145736 | tf_op jit(solution)/shard_map/ppermute | solution.py:36
  410.3 36.9 %collective-permute-start.47 = (bf16[256,2048]{1,0:T(8,128)(2,1)S(1)}, bf16[256,2048]{1,0:T(8,128)(2,1)}, u32[]{:S(2)}, u32[]{:S(2)}) collective-permute-start(bf16[256,2048]{1,0:T(8,128)(2,1)S(1)} %collective-permute-done.42.refs_2_), channel_id=1, source_target_pairs={{0,1},{1,0},{2,3},{3,2},{4,5},{5,4},{6,7},{7,6},{8,9},{9,8},{10,11... | collective-permute-start | bytes 3145736 | tf_op jit(solution)/shard_map/ppermute | solution.py:36
  428.9 18.3 %collective-permute-start.48 = (bf16[128,2048]{1,0:T(8,128)(2,1)}, bf16[128,2048]{1,0:T(8,128)(2,1)S(1)}, u32[]{:S(2)}, u32[]{:S(2)}) collective-permute-start(bf16[128,2048]{1,0:T(8,128)(2,1)} %collective-permute-done.43.refs_3_), channel_id=1, source_target_pairs={{0,1},{1,0},{2,3},{3,2},{4,5},{5,4},{6,7},{7,6},{8,9},{9,8},{10,11... | collective-permute-start | bytes 1572872 | tf_op jit(solution)/shard_map/ppermute | solution.py:36
  429.1 18.2 %collective-permute-start.49 = (bf16[128,2048]{1,0:T(8,128)(2,1)}, bf16[128,2048]{1,0:T(8,128)(2,1)S(1)}, u32[]{:S(2)}, u32[]{:S(2)}) collective-permute-start(bf16[128,2048]{1,0:T(8,128)(2,1)} %collective-permute-done.44.refs_4_), channel_id=1, source_target_pairs={{0,1},{1,0},{2,3},{3,2},{4,5},{5,4},{6,7},{7,6},{8,9},{9,8},{10,11... | collective-permute-start | bytes 1572872 | tf_op jit(solution)/shard_map/ppermute | solution.py:36
  447.1 19.8 %copy-start.17 = (f32[1,1024]{1,0:T(1,128)S(1)}, f32[1,1024]{1,0:T(1,128)}, u32[]{:S(2)}) copy-start(f32[1,1024]{1,0:T(1,128)} %get-tuple-element.76) | copy-start | bytes 12292
  447.1 19.8 %copy-start.18 = (f32[1,1024]{1,0:T(1,128)S(1)}, f32[1,1024]{1,0:T(1,128)}, u32[]{:S(2)}) copy-start(f32[1,1024]{1,0:T(1,128)} %get-tuple-element.77) | copy-start | bytes 12292
  (26 other events, 223.4 us)
Sparse Core Ops, SparseCore 0:
  212.1 187.0 all-reduce.2
